TPU v7x, 32 devices: a whole 2x2x4 slice. The times are simulated.
32 devices in a mesh: group: 8 (over z, y), proc: 4 (over x, core).
Axes of the slice: x: 2, y: 2, z: 4, core: 2. Of those that a mesh axis runs over, the one named last changes fastest.
Arguments:
- ancestor_rows: bfloat16 [32, 256, 8192], P('group', 'proc'), may hold values from -6 to 6
- piece_owner: int32 [32], replicated, may hold values from 0 to 31, each once
- structure: int32 [8, 8], replicated, may hold values from 0 to 15, as said below
- kept_blocks: int32 [8, 7], replicated, may hold values from 0 to 7, as said below
- panel_parent: bfloat16 [8, 8, 2, 256, 512], P('group', None, None, 'proc'), may hold values from -0.09375 to 0.09375
- panel_child: bfloat16 [8, 8, 2, 256, 512], P('group', None, None, 'proc'), may hold values from -0.09375 to 0.09375
- pivot_parent: bfloat16 [8, 2, 256, 512], P('group', None, 'proc'), may hold values from -4 to 6, as said below
- pivot_child: bfloat16 [8, 2, 256, 512], P('group', None, 'proc'), may hold values from -4 to 6, as said below
Outputs:
- column_parent: bfloat16 [8, 8, 2, 256, 512], P('group', None, None, 'proc')
- block_parent: bfloat16 [8, 2, 256, 512], P('group', None, 'proc')
- column_child: bfloat16 [8, 8, 2, 256, 512], P('group', None, None, 'proc')
- block_child: bfloat16 [8, 2, 256, 512], P('group', None, 'proc')
Inputs may be any that keep to these rules, and one draw needn't show every extreme that they name: `structure`: each row names 8 different top supernodes in increasing order. `kept_blocks`: each row names 7 different positions in increasing order. `piece_owner`: a permutation. `pivot_parent`: each group's block, read as a 512 x 512 matrix, is symmetric. `pivot_child`: each group's block, read as a 512 x 512 matrix, is symmetric.
All inputs are finite; a program needn't handle non-finite values.
Results may differ from a plain program's by a relative error of at most 0.018.
Values may be sent and summed in bfloat16 or wider, within the bound.
A program may use at most 128 MiB of HBM per device.

v0:
```python
import functools

import jax
import jax.numpy as jnp
from jax import lax
from jax.experimental import pallas as pl
from jax.experimental.pallas import tpu as pltpu
from jax.sharding import PartitionSpec as P


def product_kernel(strip_count, columns_ref, *refs):
    strips, panel_ref = refs[:strip_count], refs[strip_count]
    out_ref, total = refs[strip_count + 1 :]
    step = pl.program_id(0)

    @pl.when(step == 0)
    def _():
        total[...] = jnp.zeros_like(total)

    panel = panel_ref[...]
    for j, strip in enumerate(strips):
        total[j] += jnp.dot(strip[...], panel, preferred_element_type=jnp.float32)

    @pl.when(step == pl.num_programs(0) - 1)
    def _():
        out_ref[...] = total[...].astype(out_ref.dtype)


def structured_product(columns, strips, panel):
    blocks = columns.shape[0]
    rows = strips[0].shape[0]
    depth, width = panel.shape
    block = depth // blocks
    count = len(strips)
    return pl.pallas_call(
        functools.partial(product_kernel, count),
        out_shape=jax.ShapeDtypeStruct((count, rows, width), jnp.bfloat16),
        grid_spec=pltpu.PrefetchScalarGridSpec(
            num_scalar_prefetch=1,
            grid=(blocks,),
            in_specs=[pl.BlockSpec((rows, block), lambda b, c: (0, c[b]))] * count
            + [pl.BlockSpec((block, width), lambda b, c: (b, 0))],
            out_specs=pl.BlockSpec((count, rows, width), lambda b, c: (0, 0, 0)),
            scratch_shapes=[pltpu.VMEM((count, rows, width), jnp.float32)],
        ),
        compiler_params=pltpu.CompilerParams(dimension_semantics=("arbitrary",)),
        cost_estimate=pl.CostEstimate(
            flops=2 * count * rows * depth * width,
            bytes_accessed=2 * (count * rows * depth + depth * width + count * rows * width),
            transcendentals=0,
        ),
    )(columns, *strips, panel)


def unslice_kernel(pieces, in_ref, out_ref):
    procs = in_ref.shape[1]
    strip = in_ref.shape[3] // pieces
    for a in range(in_ref.shape[0]):
        slices = [in_ref[a, q] for q in range(procs)]
        out_ref[a] = jnp.concatenate(
            [x[:, c * strip : (c + 1) * strip] for c in range(pieces) for x in slices], axis=1
        )


def unslice(moved, pieces):
    count, procs, rows, slice_width = moved.shape
    step = pieces
    return pl.pallas_call(
        functools.partial(unslice_kernel, pieces),
        out_shape=jax.ShapeDtypeStruct((count, rows, procs * slice_width), moved.dtype),
        grid=(count // step,),
        in_specs=[pl.BlockSpec((step, procs, rows, slice_width), lambda i: (i, 0, 0, 0))],
        out_specs=pl.BlockSpec((step, rows, procs * slice_width), lambda i: (i, 0, 0)),
        cost_estimate=pl.CostEstimate(
            flops=0, bytes_accessed=4 * moved.size, transcendentals=0
        ),
    )(moved)


def per_device(
    groups,
    procs,
    ancestor_rows,
    piece_owner,
    structure,
    kept_blocks,
    panel_parent,
    panel_child,
    pivot_parent,
    pivot_child,
):
    f32, bf16 = jnp.float32, jnp.bfloat16
    group_index = lax.axis_index("group")
    proc_index = lax.axis_index("proc")
    owned_count, strip_rows, top_width = ancestor_rows.shape
    blocks = structure.shape[1]
    pieces = panel_parent.shape[2]
    width = panel_parent.shape[-1]
    slice_width = width // procs
    kept = kept_blocks.shape[1]
    own_structure = structure[group_index]
    kept_positions = kept_blocks[group_index]

    order = list(range(0, groups, 2)) + list(range(groups - 1, 0, -2))
    place_of = [order.index(g) for g in range(groups)]
    order_array = jnp.array(order, jnp.int32)
    place_array = jnp.array(place_of, jnp.int32)
    place = place_array[group_index]

    def shift(value, distance):
        pairs = [(order[i], order[(i + distance) % groups]) for i in range(groups)]
        return lax.ppermute(value, "group", pairs)

    def to_slices(panel):
        shape = panel.shape[:-1]
        view = panel.reshape(shape + (pieces, procs, strip_rows))
        return jnp.swapaxes(view, -3, -2).reshape(shape + (procs, slice_width))

    local_parent, local_child = panel_parent[0], panel_child[0]
    positions = jnp.arange(blocks, dtype=jnp.int32)
    match = kept_positions[None, :] == positions[:, None]
    source_block = jnp.sum(match * jnp.arange(1, kept + 1, dtype=jnp.int32)[None, :], axis=1)
    met = jnp.any(match, axis=1)
    placed_child = jnp.where(
        met[:, None, None, None], local_child[source_block], jnp.zeros((), bf16)
    )
    packed = jnp.concatenate([to_slices(local_parent), to_slices(placed_child)], axis=-1)
    panel = lax.all_to_all(packed, "proc", split_axis=3, concat_axis=2, tiled=True)
    panel = panel.reshape(blocks * width, 2 * slice_width)

    panel, ancestor_rows = lax.optimization_barrier((panel, ancestor_rows))
    strips, offsets = [ancestor_rows.reshape(owned_count * strip_rows, top_width)], [0]
    bit = procs // 2
    while bit:
        pairs = [(q, q ^ bit) for q in range(procs)]
        strips = strips + [lax.ppermute(strip, "proc", pairs) for strip in strips]
        offsets = offsets + [offset ^ bit for offset in offsets]
        bit //= 2

    last_strip, panels_after = lax.optimization_barrier(
        (strips[-1], (local_parent, local_child))
    )
    strips = strips[:-1] + [last_strip]
    local_parent, local_child = panels_after
    whole_parent = lax.all_gather(local_parent, "proc", axis=2, tiled=True).reshape(-1, width)
    whole_child = lax.all_gather(local_child, "proc", axis=2, tiled=True).reshape(-1, width)

    def send_home(arrived, distance):
        columns = structure[order_array[(place - distance) % groups]]
        product = structured_product(columns, strips, arrived)
        return shift(product, -distance)

    received = [None] * groups
    received[0] = structured_product(own_structure, strips, panel)
    forth = back = panel
    half = panel.shape[0] // 2
    for distance in range(1, groups // 2):
        forth = shift(forth, 1)
        back = shift(back, -1)
        received[distance] = send_home(forth, distance)
        received[groups - distance] = send_home(back, groups - distance)
    front, rear = forth[:half], back[half:]
    front = shift(front, 1)
    rear = shift(rear, -1)
    opposite = jnp.concatenate([front, rear], axis=0)
    received[groups // 2] = send_home(opposite, groups // 2)

    gathered = jnp.stack(received).reshape(
        groups * procs * owned_count, strip_rows, 2 * slice_width
    )
    wanted = own_structure[:, None] * pieces + jnp.arange(pieces, dtype=jnp.int32)[None, :]
    slab_index = piece_owner[wanted]
    ahead = (place_array[slab_index // owned_count] - place) % groups
    within = slab_index % owned_count
    strip_slot = {offset: j for j, offset in enumerate(offsets)}
    slot_array = jnp.array([strip_slot[offset] for offset in range(procs)], jnp.int32)
    slots = slot_array[jnp.arange(procs, dtype=jnp.int32) ^ proc_index]
    index = (ahead[:, :, None] * procs + slots[None, None, :]) * owned_count + within[:, :, None]
    products = gathered[index.reshape(-1)].reshape(
        blocks, pieces, procs, strip_rows, 2 * slice_width
    )
    column_slice = -products[..., :slice_width]
    inner_slice = products[..., slice_width:]

    def to_strips(value):
        lead = value.shape[:-3]
        moved = lax.all_to_all(
            value, "proc", split_axis=len(lead), concat_axis=len(lead), tiled=True
        )
        flat = moved.reshape((-1,) + moved.shape[-3:])
        return unslice(flat, pieces).reshape(lead + (strip_rows, width))

    both = to_strips(jnp.stack([column_slice, inner_slice]))
    column_parent, inner = both[0], both[1]

    flat_column = column_slice.reshape(blocks * width, slice_width)
    product_block = lax.dot_general(
        whole_parent, flat_column, (((0,), (0,)), ((), ())), preferred_element_type=f32
    )
    pivot_slice = pivot_parent[0].reshape(slice_width, width).T
    block_slice = (pivot_slice.astype(f32) - product_block).astype(bf16)
    block_parent = to_strips(block_slice.reshape(pieces, procs, strip_rows, slice_width))

    head_slice = jnp.concatenate(
        [
            block_slice[None],
            column_slice.reshape(blocks, width, slice_width)[kept_positions],
        ],
        axis=0,
    ).reshape(-1, slice_width)
    first_rows = lax.dot_general(
        head_slice, whole_child, (((0,), (0,)), ((), ())), preferred_element_type=f32
    ).reshape(1, pieces, strip_rows, width)

    head_rows = column_parent[kept_positions].reshape(-1, width)
    outer = jnp.dot(head_rows, whole_child[:width], preferred_element_type=f32)
    rest = outer.reshape(kept, pieces, strip_rows, width) + inner[kept_positions].astype(f32)
    column_child = (-jnp.concatenate([first_rows, rest], axis=0)).astype(bf16)

    partial = lax.dot_general(
        local_child.reshape(-1, width),
        column_child.reshape(-1, width),
        (((0,), (0,)), ((), ())),
        preferred_element_type=f32,
    ).astype(bf16)
    partial = lax.all_to_all(
        partial.reshape(pieces, procs, strip_rows, width),
        "proc",
        split_axis=1,
        concat_axis=1,
        tiled=True,
    )
    summed = jnp.sum(partial.astype(f32), axis=1)
    block_child = (pivot_child[0].astype(f32) - summed).astype(bf16)
    return column_parent[None], block_parent[None], column_child[None], block_child[None]


def solution(mesh):
    in_specs = (
        P("group", "proc", None),
        P(),
        P(),
        P(),
        P("group", None, None, "proc", None),
        P("group", None, None, "proc", None),
        P("group", None, "proc", None),
        P("group", None, "proc", None),
    )
    out_specs = (
        P("group", None, None, "proc", None),
        P("group", None, "proc", None),
        P("group", None, None, "proc", None),
        P("group", None, "proc", None),
    )
    groups = mesh.shape["group"]

    def body(*args):
        return per_device(groups, mesh.shape["proc"], *args)

    return jax.shard_map(
        body, mesh=mesh, in_specs=in_specs, out_specs=out_specs, check_vma=False
    )
```

profile of v0, /device:TPU:0, one launch (start us, length us, event | category | flops | bytes accessed | tf_op | source)
XLA Modules:
  0.0 562.4 jit_solution(18011607181783422555)
XLA Ops:
  8.2 1.8 gather_fusion
  11.2 3.5 fusion.2
  14.7 4.8 reshape.352
  19.6 2.1 reshape_squeeze.4
  21.6 3.9 copy.59
  25.6 1.8 reshape.351
  27.4 1.7 pad_maximum_fusion
  29.1 29.7 %all_to_all.30 = bf16[8,2,64,4,256]{4,2,1,0,3:T(8,128)(2,1)S(1)} all-to-all(bf16[8,2,64,4,256]{4,2,1,0,3:T(8,128)(2,1)S(1)} %pad_maximum_fusion), channel_id=1, replica_groups=mesh['group'=8,'proc'=4] {'proc'}, dimensions={3} | all-to-all | bytes 4194304 | tf_op jit(solution)/shard_map/all_to_all | solution.py:128
  58.9 2.8 copy-done.4
  62.1 91.6 %collective-permute-done.refs_1_ = bf16[256,8192]{1,0:T(8,128)(2,1)S(1)} collective-permute-done((bf16[256,8192]{1,0:T(8,128)(2,1)S(1)}, bf16[256,8192]{1,0:T(8,128)(2,1)S(1)}, u32[]{:S(2)}, u32[]{:S(2)}) %collective-permute-start) | collective-permute-done | bytes 4194336 | tf_op jit(solution)/shard_map/ppermute | solution.py:136
  153.7 2.1 copy-done.5
  157.8 5.1 collective-permute-done.2.refs_3_
  162.9 1.9 copy-done.6
  164.9 39.0 %collective-permute-done.10.refs_4_ = bf16[4096,256]{1,0:T(8,128)(2,1)} collective-permute-done((bf16[4096,256]{1,0:T(8,128)(2,1)S(1)}, bf16[4096,256]{1,0:T(8,128)(2,1)}, u32[]{:S(2)}, u32[]{:S(2)}) %collective-permute-start.10) | collective-permute-done | bytes 2097184 | tf_op jit(solution)/shard_map/ppermute | solution.py:112
  205.9 45.5 %collective-permute-done.11.refs_4_ = bf16[4096,256]{1,0:T(8,128)(2,1)} collective-permute-done((bf16[4096,256]{1,0:T(8,128)(2,1)}, bf16[4096,256]{1,0:T(8,128)(2,1)}, u32[]{:S(2)}, u32[]{:S(2)}) %collective-permute-start.11) | collective-permute-done | bytes 2097184 | tf_op jit(solution)/shard_map/ppermute | solution.py:112
  270.7 27.3 %collective-permute-done.12.refs_4_ = bf16[4096,256]{1,0:T(8,128)(2,1)} collective-permute-done((bf16[4096,256]{1,0:T(8,128)(2,1)}, bf16[4096,256]{1,0:T(8,128)(2,1)}, u32[]{:S(2)}, u32[]{:S(2)}) %collective-permute-start.12) | collective-permute-done | bytes 2097184 | tf_op jit(solution)/shard_map/ppermute | solution.py:112
  299.3 1.6 collective-permute-start.13
  300.9 2.3 slice.53
  310.4 12.1 %collective-permute-done.13 = bf16[2048,256]{1,0:T(8,128)(2,1)} collective-permute-done((bf16[2048,256]{1,0:T(8,128)(2,1)S(1)}, bf16[2048,256]{1,0:T(8,128)(2,1)}, u32[]{:S(2)}, u32[]{:S(2)}) %collective-permute-start.13) | collective-permute-done | bytes 1048608 | tf_op jit(solution)/shard_map/ppermute | solution.py:112
  322.5 3.7 collective-permute-done.9
  326.2 3.0 pad_maximum_fusion.1.refs_4_
  329.3 9.6 %shard_map.145 = bf16[4,256,256]{2,1,0:T(8,128)(2,1)} custom-call(s32[8]{0:T(128)} %get-tuple-element.21.columns_ref, bf16[256,8192]{1,0:T(8,128)(2,1)} %bitcast.134, bf16[256,8192]{1,0:T(8,128)(2,1)} %copy-done.5, bf16[256,8192]{1,0:T(8,128)(2,1)} %collective-permute-done.1.refs_2_, bf16[256,8192]{1,0:T(8,128)(2,1)} %copy-done.6, ...), custom_call_target="tpu_custom_call" | custom-call | flops 2147483648 | bytes 11010048 | tf_op jit(solution)/shard_map/pallas_call | solution.py:35
  339.2 9.3 %shard_map.144 = bf16[4,256,256]{2,1,0:T(8,128)(2,1)} custom-call(s32[8]{0:T(128)} %get-tuple-element.27.columns_ref, bf16[256,8192]{1,0:T(8,128)(2,1)} %bitcast.135, bf16[256,8192]{1,0:T(8,128)(2,1)} %copy-done.5, bf16[256,8192]{1,0:T(8,128)(2,1)} %collective-permute-done.1.refs_2_, bf16[256,8192]{1,0:T(8,128)(2,1)} %copy-done.6, ...), custom_call_target="tpu_custom_call" | custom-call | flops 2147483648 | bytes 11010048 | tf_op jit(solution)/shard_map/pallas_call | solution.py:35
  348.6 2.6 collective-permute-start.16
  351.1 9.4 %shard_map.141 = bf16[4,256,256]{2,1,0:T(8,128)(2,1)} custom-call(s32[8]{0:T(128)} %get-tuple-element.24.columns_ref, bf16[256,8192]{1,0:T(8,128)(2,1)} %bitcast.136, bf16[256,8192]{1,0:T(8,128)(2,1)} %copy-done.5, bf16[256,8192]{1,0:T(8,128)(2,1)} %collective-permute-done.1.refs_2_, bf16[256,8192]{1,0:T(8,128)(2,1)} %copy-done.6, ...), custom_call_target="tpu_custom_call" | custom-call | flops 2147483648 | bytes 11010048 | tf_op jit(solution)/shard_map/pallas_call | solution.py:35
  361.9 9.3 %shard_map.140 = bf16[4,256,256]{2,1,0:T(8,128)(2,1)} custom-call(s32[8]{0:T(128)} %get-tuple-element.25.columns_ref, bf16[256,8192]{1,0:T(8,128)(2,1)} %bitcast.137, bf16[256,8192]{1,0:T(8,128)(2,1)} %copy-done.5, bf16[256,8192]{1,0:T(8,128)(2,1)} %collective-permute-done.1.refs_2_, bf16[256,8192]{1,0:T(8,128)(2,1)} %copy-done.6, ...), custom_call_target="tpu_custom_call" | custom-call | flops 2147483648 | bytes 11010048 | tf_op jit(solution)/shard_map/pallas_call | solution.py:35
  371.2 2.6 collective-permute-start.6
  373.8 9.3 %shard_map.139 = bf16[4,256,256]{2,1,0:T(8,128)(2,1)} custom-call(s32[8]{0:T(128)} %get-tuple-element.26.columns_ref, bf16[256,8192]{1,0:T(8,128)(2,1)} %bitcast.138, bf16[256,8192]{1,0:T(8,128)(2,1)} %copy-done.5, bf16[256,8192]{1,0:T(8,128)(2,1)} %collective-permute-done.1.refs_2_, bf16[256,8192]{1,0:T(8,128)(2,1)} %copy-done.6, ...), custom_call_target="tpu_custom_call" | custom-call | flops 2147483648 | bytes 11010048 | tf_op jit(solution)/shard_map/pallas_call | solution.py:35
  383.8 9.3 %shard_map.138 = bf16[4,256,256]{2,1,0:T(8,128)(2,1)} custom-call(s32[8]{0:T(128)} %get-tuple-element.15.columns_ref, bf16[256,8192]{1,0:T(8,128)(2,1)} %bitcast.139, bf16[256,8192]{1,0:T(8,128)(2,1)} %copy-done.5, bf16[256,8192]{1,0:T(8,128)(2,1)} %collective-permute-done.1.refs_2_, bf16[256,8192]{1,0:T(8,128)(2,1)} %copy-done.6, bf16[4096,256]{1,0:T(8,128)(2,1)} %bitcast.151), custom_call_target="tpu_custom_call" | custom-call | flops 2147483648 | bytes 11010048 | tf_op jit(solution)/shard_map/pallas_call | solution.py:35
  393.1 1.9 bitcast_dynamic-update-slice_fusion.7
  395.0 9.3 %shard_map.143 = bf16[4,256,256]{2,1,0:T(8,128)(2,1)} custom-call(s32[8]{0:T(128)} %get-tuple-element.22.columns_ref, bf16[256,8192]{1,0:T(8,128)(2,1)} %bitcast.140, bf16[256,8192]{1,0:T(8,128)(2,1)} %copy-done.5, bf16[256,8192]{1,0:T(8,128)(2,1)} %collective-permute-done.1.refs_2_, bf16[256,8192]{1,0:T(8,128)(2,1)} %copy-done.6, ...), custom_call_target="tpu_custom_call" | custom-call | flops 2147483648 | bytes 11010048 | tf_op jit(solution)/shard_map/pallas_call | solution.py:35
  404.3 9.4 %shard_map.142 = bf16[4,256,256]{2,1,0:T(8,128)(2,1)} custom-call(s32[8]{0:T(128)} %get-tuple-element.23.columns_ref, bf16[256,8192]{1,0:T(8,128)(2,1)} %bitcast.141, bf16[256,8192]{1,0:T(8,128)(2,1)} %copy-done.5, bf16[256,8192]{1,0:T(8,128)(2,1)} %collective-permute-done.1.refs_2_, bf16[256,8192]{1,0:T(8,128)(2,1)} %copy-done.6, ...), custom_call_target="tpu_custom_call" | custom-call | flops 2147483648 | bytes 11010048 | tf_op jit(solution)/shard_map/pallas_call | solution.py:35
  413.7 14.1 %collective-permute-done.4 = bf16[4,256,256]{2,1,0:T(8,128)(2,1)S(1)} collective-permute-done((bf16[4,256,256]{2,1,0:T(8,128)(2,1)}, bf16[4,256,256]{2,1,0:T(8,128)(2,1)S(1)}, u32[]{:S(2)}, u32[]{:S(2)}) %collective-permute-start.4) | collective-permute-done | bytes 524320 | tf_op jit(solution)/shard_map/ppermute | solution.py:112
  427.8 3.3 collective-permute-start.14
  433.7 11.9 %collective-permute-done.14 = bf16[4,256,256]{2,1,0:T(8,128)(2,1)S(1)} collective-permute-done((bf16[4,256,256]{2,1,0:T(8,128)(2,1)}, bf16[4,256,256]{2,1,0:T(8,128)(2,1)S(1)}, u32[]{:S(2)}, u32[]{:S(2)}) %collective-permute-start.14) | collective-permute-done | bytes 524320 | tf_op jit(solution)/shard_map/ppermute | solution.py:112
  446.4 27.6 %collective-permute-done.15 = bf16[4,256,256]{2,1,0:T(8,128)(2,1)S(1)} collective-permute-done((bf16[4,256,256]{2,1,0:T(8,128)(2,1)S(1)}, bf16[4,256,256]{2,1,0:T(8,128)(2,1)S(1)}, u32[]{:S(2)}, u32[]{:S(2)}) %collective-permute-start.15) | collective-permute-done | bytes 524320 | tf_op jit(solution)/shard_map/ppermute | solution.py:112
  476.5 2.9 gather_fusion.4
  481.5 3.7 all-to-all-start.1
  487.7 1.6 gather_fusion.5
  489.3 21.5 %all-to-all-done.1 = bf16[2,8,2,4,64,128]{5,4,2,1,0,3:T(8,128)(2,1)S(1)} async-done(((bf16[2,8,2,4,64,128]{5,4,2,1,0,3:T(8,128)(2,1)}), bf16[2,8,2,4,64,128]{5,4,2,1,0,3:T(8,128)(2,1)S(1)}, u32[]{:S(2)}, u32[]{:S(2)}) %all-to-all-start.1) | async-done | bytes 2097184 | tf_op jit(solution)/shard_map/all_to_all | solution.py:187
  512.4 10.0 %shard_map.146 = bf16[32,64,512]{2,1,0:T(8,128)(2,1)} custom-call(bf16[32,4,64,128]{3,2,1,0:T(8,128)(2,1)} %bitcast.148), custom_call_target="tpu_custom_call" | custom-call | bytes 4194304 | tf_op jit(solution)/shard_map/pallas_call | solution.py:68
  522.4 1.7 fusion.29
  527.2 3.6 fusion.4
  532.1 3.3 all-to-all-start.2
  535.5 3.1 fusion.31
  542.5 3.5 all-to-all-start.3
  548.0 1.7 shard_map.147
  549.6 5.2 all-to-all-done.3
  (126 shorter events, 41.9 us)
Async XLA Ops:
  7.2 261.9 %copy-start = (s32[32]{0:T(128)S(1)}, s32[32]{0:T(128)}, u32[]{:S(2)}) copy-start(s32[32]{0:T(128)} %param.12) | copy-start | bytes 388
  7.2 520.0 %all-gather.3.cloned.1.call-start = ((), (), s32[]{:S(2)}) async-start(), calls=%async_computation.4 | async-start | bytes 5242880 | tf_op jit(solution)/shard_map/all_gather | solution.py:145
  14.7 4.8 copy-start.8
  25.6 1.8 copy-start.10
  58.8 2.9 copy-start.4
  58.8 194.6 %copy-start.2 = (s32[8]{0:T(128)S(1)}, s32[8]{0:T(128)}, u32[]{:S(2)}) copy-start(s32[8]{0:T(128)} %constant.129.clone) | copy-start | bytes 100
  58.8 199.9 %copy-start.18 = (s32[8]{0:T(128)S(1)}, s32[8]{0:T(128)}, u32[]{:S(2)}) copy-start(s32[8]{0:T(128)} %constant.128.clone) | copy-start | bytes 100
  58.8 209.6 %copy-start.19 = (s32[8,8]{1,0:T(8,128)S(1)}, s32[8,8]{1,0:T(8,128)}, u32[]{:S(2)}) copy-start(s32[8,8]{1,0:T(8,128)} %param.13) | copy-start | bytes 772
  58.9 244.2 %copy-start.7 = (bf16[8,2,4,64,1,256]{5,3,2,1,0,4:T(8,128)(2,1)}, bf16[8,2,4,64,1,256]{5,3,2,1,0,4:T(8,128)(2,1)S(1)}, u32[]{:S(2)}) copy-start(bf16[8,2,4,64,1,256]{5,3,2,1,0,4:T(8,128)(2,1)S(1)} %copy.45) | copy-start | bytes 6291460
  61.7 91.9 %collective-permute-start = (bf16[256,8192]{1,0:T(8,128)(2,1)S(1)}, bf16[256,8192]{1,0:T(8,128)(2,1)S(1)}, u32[]{:S(2)}, u32[]{:S(2)}) collective-permute-start(bf16[256,8192]{1,0:T(8,128)(2,1)S(1)} %bitcast.142), channel_id=1, source_target_pairs={{0,2},{1,3},{2,0},{3,1},{4,6},{5,7},{6,4},{7,5},{8,10},{9,11},{10,... | collective-permute-start | bytes 12582920 | tf_op jit(solution)/shard_map/ppermute | solution.py:136
  153.7 2.1 copy-start.5
  155.7 7.2 %collective-permute-start.2 = (bf16[256,8192]{1,0:T(8,128)(2,1)S(1)}, bf16[256,8192]{1,0:T(8,128)(2,1)S(1)}, u32[]{:S(2)}, u32[]{:S(2)}) collective-permute-start(bf16[256,8192]{1,0:T(8,128)(2,1)S(1)} %collective-permute-done.refs_1_), channel_id=1, source_target_pairs={{0,1},{1,0},{2,3},{3,2},{4,5},{5,4},{6,7},{7,6},{8,9},{9,8},{10,11... | collective-permute-start | bytes 12582920 | tf_op jit(solution)/shard_map/ppermute | solution.py:136
  155.7 48.1 %collective-permute-start.10 = (bf16[4096,256]{1,0:T(8,128)(2,1)S(1)}, bf16[4096,256]{1,0:T(8,128)(2,1)}, u32[]{:S(2)}, u32[]{:S(2)}) collective-permute-start(bf16[4096,256]{1,0:T(8,128)(2,1)S(1)} %bitcast.149), channel_id=1, source_target_pairs={{0,4},{8,0},{16,8},{24,16},{28,24},{20,28},{12,20},{4,12},{1,5},{9... | collective-permute-start | bytes 6291464 | tf_op jit(solution)/shard_map/ppermute | solution.py:112
  157.2 48.2 %collective-permute-start.3 = (bf16[4096,256]{1,0:T(8,128)(2,1)S(1)}, bf16[4096,256]{1,0:T(8,128)(2,1)}, u32[]{:S(2)}, u32[]{:S(2)}) collective-permute-start(bf16[4096,256]{1,0:T(8,128)(2,1)S(1)} %bitcast.150), channel_id=1, source_target_pairs={{0,8},{8,16},{16,24},{24,28},{28,20},{20,12},{12,4},{4,0},{1,9},{9... | collective-permute-start | bytes 6291464 | tf_op jit(solution)/shard_map/ppermute | solution.py:112
  162.9 1.9 copy-start.6
  164.8 370.6 %all-gather.5.cloned.1.call-start = ((), (), s32[]{:S(2)}) async-start(), calls=%async_computation.5 | async-start | bytes 5242880 | tf_op jit(solution)/shard_map/all_gather | solution.py:146
  203.9 47.5 %collective-permute-start.11 = (bf16[4096,256]{1,0:T(8,128)(2,1)}, bf16[4096,256]{1,0:T(8,128)(2,1)}, u32[]{:S(2)}, u32[]{:S(2)}) collective-permute-start(bf16[4096,256]{1,0:T(8,128)(2,1)} %collective-permute-done.10.refs_4_), channel_id=1, source_target_pairs={{0,4},{8,0},{16,8},{24,16},{28,24},{20,28},{12,20},{4,12},{1,5},{9... | collective-permute-start | bytes 6291464 | tf_op jit(solution)/shard_map/ppermute | solution.py:112
  205.4 47.5 %collective-permute-start.5 = (bf16[4096,256]{1,0:T(8,128)(2,1)}, bf16[4096,256]{1,0:T(8,128)(2,1)}, u32[]{:S(2)}, u32[]{:S(2)}) collective-permute-start(bf16[4096,256]{1,0:T(8,128)(2,1)} %collective-permute-done.3.refs_4_), channel_id=1, source_target_pairs={{0,8},{8,16},{16,24},{24,28},{28,20},{20,12},{12,4},{4,0},{1,9},{9... | collective-permute-start | bytes 6291464 | tf_op jit(solution)/shard_map/ppermute | solution.py:112
  205.9 123.3 %collective-permute-start.1 = (bf16[256,8192]{1,0:T(8,128)(2,1)}, bf16[256,8192]{1,0:T(8,128)(2,1)}, u32[]{:S(2)}, u32[]{:S(2)}) collective-permute-start(bf16[256,8192]{1,0:T(8,128)(2,1)} %bitcast.133), channel_id=1, source_target_pairs={{0,1},{1,0},{2,3},{3,2},{4,5},{5,4},{6,7},{7,6},{8,9},{9,8},{10,11... | collective-permute-start | bytes 12582920 | tf_op jit(solution)/shard_map/ppermute | solution.py:136
  251.4 46.6 %collective-permute-start.12 = (bf16[4096,256]{1,0:T(8,128)(2,1)}, bf16[4096,256]{1,0:T(8,128)(2,1)}, u32[]{:S(2)}, u32[]{:S(2)}) collective-permute-start(bf16[4096,256]{1,0:T(8,128)(2,1)} %collective-permute-done.11.refs_4_), channel_id=1, source_target_pairs={{0,4},{8,0},{16,8},{24,16},{28,24},{20,28},{12,20},{4,12},{1,5},{9... | collective-permute-start | bytes 6291464 | tf_op jit(solution)/shard_map/ppermute | solution.py:112
  252.9 48.0 %collective-permute-start.7 = (bf16[4096,256]{1,0:T(8,128)(2,1)}, bf16[4096,256]{1,0:T(8,128)(2,1)}, u32[]{:S(2)}, u32[]{:S(2)}) collective-permute-start(bf16[4096,256]{1,0:T(8,128)(2,1)} %collective-permute-done.5.refs_4_), channel_id=1, source_target_pairs={{0,8},{8,16},{16,24},{24,28},{28,20},{20,12},{12,4},{4,0},{1,9},{9... | collective-permute-start | bytes 6291464 | tf_op jit(solution)/shard_map/ppermute | solution.py:112
  270.7 33.7 %copy-start.3 = (s32[4]{0:T(128)S(1)}, s32[4]{0:T(128)}, u32[]{:S(2)}) copy-start(s32[4]{0:T(128)} %constant.130.clone) | copy-start | bytes 52
  299.3 23.2 %collective-permute-start.13 = (bf16[2048,256]{1,0:T(8,128)(2,1)S(1)}, bf16[2048,256]{1,0:T(8,128)(2,1)}, u32[]{:S(2)}, u32[]{:S(2)}) collective-permute-start(bf16[2048,256]{1,0:T(8,128)(2,1)S(1)} %slice.54), channel_id=1, source_target_pairs={{0,4},{8,0},{16,8},{24,16},{28,24},{20,28},{12,20},{4,12},{1,5},{9... | collective-permute-start | bytes 3145736 | tf_op jit(solution)/shard_map/ppermute | solution.py:112
  303.2 23.0 %collective-permute-start.9 = (bf16[2048,256]{1,0:T(8,128)(2,1)}, bf16[2048,256]{1,0:T(8,128)(2,1)}, u32[]{:S(2)}, u32[]{:S(2)}) collective-permute-start(bf16[2048,256]{1,0:T(8,128)(2,1)} %slice.53), channel_id=1, source_target_pairs={{0,8},{8,16},{16,24},{24,28},{28,20},{20,12},{12,4},{4,0},{1,9},{9... | collective-permute-start | bytes 3145736 | tf_op jit(solution)/shard_map/ppermute | solution.py:112
  338.8 136.8 %collective-permute-start.17 = (bf16[4,256,256]{2,1,0:T(8,128)(2,1)}, bf16[4,256,256]{2,1,0:T(8,128)(2,1)S(1)}, u32[]{:S(2)}, u32[]{:S(2)}) collective-permute-start(bf16[4,256,256]{2,1,0:T(8,128)(2,1)} %shard_map.145), channel_id=1, source_target_pairs={{0,8},{8,16},{16,24},{24,28},{28,20},{20,12},{12,4},{4,0},{1,9},{9... | collective-permute-start | bytes 1572872 | tf_op jit(solution)/shard_map/ppermute | solution.py:112
  348.6 126.2 %collective-permute-start.16 = (bf16[4,256,256]{2,1,0:T(8,128)(2,1)}, bf16[4,256,256]{2,1,0:T(8,128)(2,1)S(1)}, u32[]{:S(2)}, u32[]{:S(2)}) collective-permute-start(bf16[4,256,256]{2,1,0:T(8,128)(2,1)} %shard_map.144), channel_id=1, source_target_pairs={{0,16},{8,24},{16,28},{24,20},{28,12},{20,4},{12,0},{4,8},{1,17},{... | collective-permute-start | bytes 1572872 | tf_op jit(solution)/shard_map/ppermute | solution.py:112
  360.5 72.3 %collective-permute-start.8 = (bf16[4,256,256]{2,1,0:T(8,128)(2,1)}, bf16[4,256,256]{2,1,0:T(8,128)(2,1)S(1)}, u32[]{:S(2)}, u32[]{:S(2)}) collective-permute-start(bf16[4,256,256]{2,1,0:T(8,128)(2,1)} %shard_map.141), channel_id=1, source_target_pairs={{0,20},{8,12},{16,4},{24,0},{28,8},{20,16},{12,24},{4,28},{1,21},{... | collective-permute-start | bytes 1572872 | tf_op jit(solution)/shard_map/ppermute | solution.py:112
  371.2 60.8 %collective-permute-start.6 = (bf16[4,256,256]{2,1,0:T(8,128)(2,1)}, bf16[4,256,256]{2,1,0:T(8,128)(2,1)S(1)}, u32[]{:S(2)}, u32[]{:S(2)}) collective-permute-start(bf16[4,256,256]{2,1,0:T(8,128)(2,1)} %shard_map.140), channel_id=1, source_target_pairs={{0,12},{8,4},{16,0},{24,8},{28,16},{20,24},{12,28},{4,20},{1,13},{... | collective-permute-start | bytes 1572872 | tf_op jit(solution)/shard_map/ppermute | solution.py:112
  383.1 44.7 %collective-permute-start.4 = (bf16[4,256,256]{2,1,0:T(8,128)(2,1)}, bf16[4,256,256]{2,1,0:T(8,128)(2,1)S(1)}, u32[]{:S(2)}, u32[]{:S(2)}) collective-permute-start(bf16[4,256,256]{2,1,0:T(8,128)(2,1)} %shard_map.139), channel_id=1, source_target_pairs={{0,4},{8,0},{16,8},{24,16},{28,24},{20,28},{12,20},{4,12},{1,5},{9... | collective-permute-start | bytes 1572872 | tf_op jit(solution)/shard_map/ppermute | solution.py:112
  404.3 27.7 %copy-start.15 = (bf16[4,256,256]{2,1,0:T(8,128)(2,1)S(1)}, bf16[4,256,256]{2,1,0:T(8,128)(2,1)}, u32[]{:S(2)}) copy-start(bf16[4,256,256]{2,1,0:T(8,128)(2,1)} %shard_map.143) | copy-start | bytes 1572868
  427.8 17.8 %collective-permute-start.14 = (bf16[4,256,256]{2,1,0:T(8,128)(2,1)}, bf16[4,256,256]{2,1,0:T(8,128)(2,1)S(1)}, u32[]{:S(2)}, u32[]{:S(2)}) collective-permute-start(bf16[4,256,256]{2,1,0:T(8,128)(2,1)} %shard_map.142), channel_id=1, source_target_pairs={{0,28},{8,20},{16,12},{24,4},{28,0},{20,8},{12,16},{4,24},{1,29},{... | collective-permute-start | bytes 1572872 | tf_op jit(solution)/shard_map/ppermute | solution.py:112
  432.0 42.0 %collective-permute-start.15 = (bf16[4,256,256]{2,1,0:T(8,128)(2,1)S(1)}, bf16[4,256,256]{2,1,0:T(8,128)(2,1)S(1)}, u32[]{:S(2)}, u32[]{:S(2)}) collective-permute-start(bf16[4,256,256]{2,1,0:T(8,128)(2,1)S(1)} %copy-done.15), channel_id=1, source_target_pairs={{0,24},{8,28},{16,20},{24,12},{28,4},{20,0},{12,8},{4,16},{1,25},{... | collective-permute-start | bytes 1572872 | tf_op jit(solution)/shard_map/ppermute | solution.py:112
  481.5 3.8 copy-start.16
  481.5 29.4 %all-to-all-start.1 = ((bf16[2,8,2,4,64,128]{5,4,2,1,0,3:T(8,128)(2,1)}), bf16[2,8,2,4,64,128]{5,4,2,1,0,3:T(8,128)(2,1)S(1)}, u32[]{:S(2)}, u32[]{:S(2)}) async-start(bf16[2,8,2,4,64,128]{5,4,2,1,0,3:T(8,128)(2,1)} %copy.46), calls=%async_computation.1 | async-start | bytes 4194304 | tf_op jit(solution)/shard_map/all_to_all | solution.py:187
  524.1 6.7 %copy-start.11 = (bf16[16,64,512]{2,1,0:T(8,128)(2,1)}, bf16[16,64,512]{2,1,0:T(8,128)(2,1)S(1)}, u32[]{:S(2)}) copy-start(bf16[16,64,512]{2,1,0:T(8,128)(2,1)S(1)} %get-tuple-element.17) | copy-start | bytes 3145732
  527.2 3.6 copy-start.12
  532.1 10.4 %all-to-all-start.2 = ((bf16[2,4,64,128]{3,2,0,1:T(8,128)(2,1)}), bf16[2,4,64,128]{3,2,0,1:T(8,128)(2,1)S(1)}, u32[]{:S(2)}, u32[]{:S(2)}) async-start(bf16[2,4,64,128]{3,2,0,1:T(8,128)(2,1)} %copy.49), calls=%async_computation.2 | async-start | bytes 262144 | tf_op jit(solution)/shard_map/all_to_all | solution.py:187
  535.5 4.2 copy-start.13
  535.5 4.2 copy-start.14
  539.7 1.2 copy-start.9
  542.5 12.3 %all-to-all-start.3 = ((bf16[2,4,64,512]{3,2,0,1:T(8,128)(2,1)}), bf16[2,4,64,512]{3,2,0,1:T(8,128)(2,1)S(1)}, u32[]{:S(2)}, u32[]{:S(2)}) async-start(bf16[2,4,64,512]{3,2,0,1:T(8,128)(2,1)} %copy.52), calls=%async_computation.3 | async-start | bytes 1048576 | tf_op jit(solution)/shard_map/all_to_all | solution.py:226
  546.0 9.6 %copy-start.1 = (s32[32]{0:T(128)S(1)}, s32[32]{0:T(128)}, u32[]{:S(2)}) copy-start(s32[32]{0:T(128)} %param.12) | copy-start | bytes 388
  546.0 8.8 %copy-start.17 = (bf16[1,2,64,512]{3,2,1,0:T(8,128)(2,1)S(1)}, bf16[1,2,64,512]{3,2,1,0:T(8,128)(2,1)}, u32[]{:S(2)}) copy-start(bf16[1,2,64,512]{3,2,1,0:T(8,128)(2,1)} %param.18) | copy-start | bytes 393220
Sparse Core Ops, SparseCore 0:
  165.0 35.0 all-gather.2
  329.4 34.0 all-gather.4
where the time goes:
time: 565 us; the launch traced here: 562 us
  waiting for transfers between devices  305 us (54%)
  Pallas kernels  86.6 us (15%)
  local copies, waits for them, and re-layouts  56.7 us (10%)
  between operations  32.7 us (6%)
  starting transfers between devices  30.1 us (5%)
  blocking collectives  29.7 us (5%)
  other arithmetic  14 us (2%)
  matrix products  8.05 us (1%)
    ppermute x15, waiting for transfers between devices, shift(): return lax.ppermute(value, 'group', pairs)  181 us
    ppermute x3, waiting for transfers between devices, per_device(): strips = strips + [lax.ppermute(strip, 'proc', pairs) for strip in strips]  96.7 us
    pallas_call x8, Pallas kernels, structured_product(): pl.pallas_call(functools.partial(product_kernel, count), out_shape=jax.Sh...  74.9 us
    all_to_all x1, blocking collectives, per_device(): lax.all_to_all(packed, 'proc', split_axis=3, concat_axis=2, tiled=True)  29.7 us
    all_to_all x2, waiting for transfers between devices, to_strips(): lax.all_to_all(value, 'proc', split_axis=len(lead), concat_axis=len(lead)...  21.5 us
    ppermute x15, starting transfers between devices, shift(): return lax.ppermute(value, 'group', pairs)  19.1 us
    unnamed x47, local copies, waits for them, and re-layouts  14.4 us
    pallas_call x2, Pallas kernels, unslice(): pl.pallas_call(functools.partial(unslice_kernel, pieces), out_shape=jax.S...  11.7 us
  transfers between devices with their start and end apart: 23, of which 12 were waited for; matrix products, arithmetic and copies ran while one was open for 9% of the time, Pallas kernels for 15%

commit v1 on v0

--- a/solution.py
+++ b/solution.py
@@ -1,4 +1,5 @@
 import functools
+import math
 
 import jax
 import jax.numpy as jnp
@@ -52,6 +53,47 @@
     )(columns, *strips, panel)
 
 
+def pack_kernel(source_ref, met_ref, parent_ref, child_ref, out_ref):
+    pieces, _, width = parent_ref.shape[1:]
+    procs = out_ref.shape[0]
+    part = width // (pieces * procs)
+    met = met_ref[pl.program_id(0)] > 0
+    for a in range(pieces):
+        parent = parent_ref[0, a]
+        child = child_ref[0, a]
+        child = jnp.where(met, child, jnp.zeros_like(child))
+        for q in range(procs):
+            out_ref[q, 0, a] = jnp.concatenate(
+                [
+                    panel[:, (c * procs + q) * part : (c * procs + q + 1) * part]
+                    for panel in (parent, child)
+                    for c in range(pieces)
+                ],
+                axis=1,
+            )
+
+
+def pack(source_block, met, parent, child, procs):
+    blocks, pieces, strip, width = parent.shape
+    return pl.pallas_call(
+        pack_kernel,
+        out_shape=jax.ShapeDtypeStruct(
+            (procs, blocks, pieces, strip, 2 * width // procs), parent.dtype
+        ),
+        grid_spec=pltpu.PrefetchScalarGridSpec(
+            num_scalar_prefetch=2,
+            grid=(blocks,),
+            in_specs=[
+                pl.BlockSpec((1, pieces, strip, width), lambda b, s, m: (b, 0, 0, 0)),
+                pl.BlockSpec((1, pieces, strip, width), lambda b, s, m: (s[b], 0, 0, 0)),
+            ],
+            out_specs=pl.BlockSpec(
+                (procs, 1, pieces, strip, 2 * width // procs), lambda b, s, m: (0, b, 0, 0, 0)
+            ),
+        ),
+    )(source_block, met, parent, child)
+
+
 def unslice_kernel(pieces, in_ref, out_ref):
     procs = in_ref.shape[1]
     strip = in_ref.shape[3] // pieces
@@ -64,7 +106,7 @@
 
 def unslice(moved, pieces):
     count, procs, rows, slice_width = moved.shape
-    step = pieces
+    step = math.gcd(count, 8)
     return pl.pallas_call(
         functools.partial(unslice_kernel, pieces),
         out_shape=jax.ShapeDtypeStruct((count, rows, procs * slice_width), moved.dtype),
@@ -111,21 +153,16 @@
         pairs = [(order[i], order[(i + distance) % groups]) for i in range(groups)]
         return lax.ppermute(value, "group", pairs)
 
-    def to_slices(panel):
-        shape = panel.shape[:-1]
-        view = panel.reshape(shape + (pieces, procs, strip_rows))
-        return jnp.swapaxes(view, -3, -2).reshape(shape + (procs, slice_width))
-
     local_parent, local_child = panel_parent[0], panel_child[0]
     positions = jnp.arange(blocks, dtype=jnp.int32)
     match = kept_positions[None, :] == positions[:, None]
     source_block = jnp.sum(match * jnp.arange(1, kept + 1, dtype=jnp.int32)[None, :], axis=1)
     met = jnp.any(match, axis=1)
-    placed_child = jnp.where(
-        met[:, None, None, None], local_child[source_block], jnp.zeros((), bf16)
-    )
-    packed = jnp.concatenate([to_slices(local_parent), to_slices(placed_child)], axis=-1)
-    panel = lax.all_to_all(packed, "proc", split_axis=3, concat_axis=2, tiled=True)
+    packed = pack(
+        source_block.astype(jnp.int32), met.astype(jnp.int32), local_parent, local_child, procs
+    )
+    panel = lax.all_to_all(packed, "proc", split_axis=0, concat_axis=0, tiled=True)
+    panel = jnp.moveaxis(panel, 0, 2)
     panel = panel.reshape(blocks * width, 2 * slice_width)
 
     panel, ancestor_rows = lax.optimization_barrier((panel, ancestor_rows))
@@ -133,17 +170,12 @@
     bit = procs // 2
     while bit:
         pairs = [(q, q ^ bit) for q in range(procs)]
-        strips = strips + [lax.ppermute(strip, "proc", pairs) for strip in strips]
+        arrived = []
+        for strip in strips:
+            arrived.append(lax.ppermute(strip, "proc", pairs))
+        strips = strips + arrived
         offsets = offsets + [offset ^ bit for offset in offsets]
         bit //= 2
-
-    last_strip, panels_after = lax.optimization_barrier(
-        (strips[-1], (local_parent, local_child))
-    )
-    strips = strips[:-1] + [last_strip]
-    local_parent, local_child = panels_after
-    whole_parent = lax.all_gather(local_parent, "proc", axis=2, tiled=True).reshape(-1, width)
-    whole_child = lax.all_gather(local_child, "proc", axis=2, tiled=True).reshape(-1, width)
 
     def send_home(arrived, distance):
         columns = structure[order_array[(place - distance) % groups]]
@@ -152,6 +184,12 @@
 
     received = [None] * groups
     received[0] = structured_product(own_structure, strips, panel)
+    received[0], panels_after = lax.optimization_barrier(
+        (received[0], (local_parent, local_child))
+    )
+    local_parent, local_child = panels_after
+    whole_parent = lax.all_gather(local_parent, "proc", axis=2, tiled=True).reshape(-1, width)
+    whole_child = lax.all_gather(local_child, "proc", axis=2, tiled=True).reshape(-1, width)
     forth = back = panel
     half = panel.shape[0] // 2
     for distance in range(1, groups // 2):

time: 565 us -> 519 us (0.919)
  waiting for transfers between devices: 305 us -> 274 us
  local copies, waits for them, and re-layouts: 56.7 us -> 36.9 us
    ppermute x15, waiting for transfers between devices: 181 us -> 152 us  [shift(): return lax.ppermute(value, 'group', pairs)]
    pallas_call x0 -> x1, Pallas kernels: none -> 6.94 us  [pack(): pl.pallas_call(pack_kernel, out_shape=jax.ShapeDtypeStruct((procs, blocks...]
    reshape x2 -> x0, local copies, waits for them, and re-layouts: 6.62 us -> none  [to_slices(): return jnp.swapaxes(view, -3, -2).reshape(shape + (procs, slice_width))]
    another operation x2 -> x0, local copies, waits for them, and re-layouts: 6.01 us -> none  [to_slices(): view = panel.reshape(shape + (pieces, procs, strip_rows))]
    pallas_call x2, Pallas kernels: 11.7 us -> 5.81 us  [unslice(): pl.pallas_call(functools.partial(unslice_kernel, pieces), out_shape=jax.S...]
  transfers between devices with their start and end apart: 23 -> 23, of which waited for: 12 -> 11; matrix products, arithmetic and copies ran while one was open for 9% -> 9% of each run, Pallas kernels for 15% -> 16%
where the time goes in v1:
time: 519 us; the launch traced here: 511 us
  waiting for transfers between devices  274 us (53%)
  Pallas kernels  88.1 us (17%)
  local copies, waits for them, and re-layouts  36.9 us (7%)
  between operations  33 us (6%)
  blocking collectives  30 us (6%)
  starting transfers between devices  29.9 us (6%)
  other arithmetic  10.9 us (2%)
  matrix products  7.99 us (2%)
    ppermute x15, waiting for transfers between devices, shift(): return lax.ppermute(value, 'group', pairs)  152 us
    ppermute x3, waiting for transfers between devices, per_device(): arrived.append(lax.ppermute(strip, 'proc', pairs))  95.8 us
    pallas_call x8, Pallas kernels, structured_product(): pl.pallas_call(functools.partial(product_kernel, count), out_shape=jax.Sh...  75.3 us
    all_to_all x1, blocking collectives, per_device(): lax.all_to_all(packed, 'proc', split_axis=0, concat_axis=0, tiled=True)  30 us
    all_to_all x2, waiting for transfers between devices, to_strips(): lax.all_to_all(value, 'proc', split_axis=len(lead), concat_axis=len(lead)...  21.5 us
    ppermute x15, starting transfers between devices, shift(): return lax.ppermute(value, 'group', pairs)  18.7 us
    unnamed x47, local copies, waits for them, and re-layouts  11.3 us
  transfers between devices with their start and end apart: 23, of which 11 were waited for; matrix products, arithmetic and copies ran while one was open for 9% of the time, Pallas kernels for 16%

profile of v1, /device:TPU:0, one launch (start us, length us, event | category | flops | bytes accessed | tf_op | source)
XLA Modules:
  0.0 511.1 jit_solution(1213562918685399541)
XLA Ops:
  9.2 6.9 %shard_map.138 = bf16[4,8,2,64,256]{4,3,2,1,0:T(8,128)(2,1)} custom-call(s32[8]{0:T(128)} %select_reduce_fusion.source_ref, s32[8]{0:T(128)} %convert_element_type.45.met_ref, bf16[8,2,64,512]{3,2,1,0:T(8,128)(2,1)} %bitcast.135, bf16[8,2,64,512]{3,2,1,0:T(8,128)(2,1)} %bitcast.137), custom_call_target="tpu_custom_call" | custom-call | tf_op jit(solution)/shard_map/pallas_call | solution.py:78
  16.1 30.0 %all_to_all.20 = bf16[4,8,2,64,256]{4,3,2,1,0:T(8,128)(2,1)S(1)} all-to-all(bf16[4,8,2,64,256]{4,3,2,1,0:T(8,128)(2,1)} %shard_map.138), channel_id=1, replica_groups=mesh['group'=8,'proc'=4] {'proc'}, dimensions={0} | all-to-all | bytes 4194304 | tf_op jit(solution)/shard_map/all_to_all | solution.py:164
  46.3 2.8 copy-done.4
  49.5 91.6 %collective-permute-done.refs_1_ = bf16[256,8192]{1,0:T(8,128)(2,1)S(1)} collective-permute-done((bf16[256,8192]{1,0:T(8,128)(2,1)S(1)}, bf16[256,8192]{1,0:T(8,128)(2,1)S(1)}, u32[]{:S(2)}, u32[]{:S(2)}) %collective-permute-start) | collective-permute-done | bytes 4194336 | tf_op jit(solution)/shard_map/ppermute | solution.py:175
  141.1 2.3 collective-permute-start.10
  144.0 4.2 collective-permute-done.2.refs_3_
  148.2 2.0 copy-done.7
  150.2 9.4 %shard_map.139 = bf16[4,256,256]{2,1,0:T(8,128)(2,1)} custom-call(s32[8]{0:T(128)} %get-tuple-element.15.columns_ref, bf16[256,8192]{1,0:T(8,128)(2,1)} %bitcast.114, bf16[256,8192]{1,0:T(8,128)(2,1)} %copy-done.5, bf16[256,8192]{1,0:T(8,128)(2,1)} %copy-done.6, bf16[256,8192]{1,0:T(8,128)(2,1)} %copy-done.7, bf16[4096,256]{1,0:T(8,128)(2,1)} %bitcast.131), custom_call_target="tpu_custom_call" | custom-call | flops 2147483648 | bytes 11010048 | tf_op jit(solution)/shard_map/pallas_call | solution.py:36
  159.7 30.1 %collective-permute-done.10.refs_4_ = bf16[4096,256]{1,0:T(8,128)(2,1)} collective-permute-done((bf16[4096,256]{1,0:T(8,128)(2,1)S(1)}, bf16[4096,256]{1,0:T(8,128)(2,1)}, u32[]{:S(2)}, u32[]{:S(2)}) %collective-permute-start.10) | collective-permute-done | bytes 2097184 | tf_op jit(solution)/shard_map/ppermute | solution.py:154
  189.9 1.7 collective-permute-start.11
  191.9 45.7 %collective-permute-done.11.refs_4_ = bf16[4096,256]{1,0:T(8,128)(2,1)} collective-permute-done((bf16[4096,256]{1,0:T(8,128)(2,1)}, bf16[4096,256]{1,0:T(8,128)(2,1)}, u32[]{:S(2)}, u32[]{:S(2)}) %collective-permute-start.11) | collective-permute-done | bytes 2097184 | tf_op jit(solution)/shard_map/ppermute | solution.py:154
  237.7 1.4 collective-permute-start.12
  242.6 41.8 %collective-permute-done.12.refs_4_ = bf16[4096,256]{1,0:T(8,128)(2,1)S(1)} collective-permute-done((bf16[4096,256]{1,0:T(8,128)(2,1)}, bf16[4096,256]{1,0:T(8,128)(2,1)S(1)}, u32[]{:S(2)}, u32[]{:S(2)}) %collective-permute-start.12) | collective-permute-done | bytes 2097184 | tf_op jit(solution)/shard_map/ppermute | solution.py:154
  284.5 1.2 collective-permute-start.13
  285.7 2.3 slice.51
  309.8 1.3 collective-permute-done.9
  311.1 3.0 pad_maximum_fusion.refs_4_
  314.2 9.7 %shard_map.140 = bf16[4,256,256]{2,1,0:T(8,128)(2,1)} custom-call(s32[8]{0:T(128)} %get-tuple-element.26.columns_ref, bf16[256,8192]{1,0:T(8,128)(2,1)} %bitcast.115, bf16[256,8192]{1,0:T(8,128)(2,1)} %copy-done.5, bf16[256,8192]{1,0:T(8,128)(2,1)} %copy-done.6, bf16[256,8192]{1,0:T(8,128)(2,1)} %copy-done.7, bf16[4096,256]{1,0:T(8,128)(2,1)} %collective-permute-done.3.refs_4_), custom_call_target="tpu_custom_call" | custom-call | flops 2147483648 | bytes 11010048 | tf_op jit(solution)/shard_map/pallas_call | solution.py:36
  323.8 1.7 collective-permute-start.4
  325.5 9.3 %shard_map.141 = bf16[4,256,256]{2,1,0:T(8,128)(2,1)} custom-call(s32[8]{0:T(128)} %get-tuple-element.25.columns_ref, bf16[256,8192]{1,0:T(8,128)(2,1)} %bitcast.116, bf16[256,8192]{1,0:T(8,128)(2,1)} %copy-done.5, bf16[256,8192]{1,0:T(8,128)(2,1)} %copy-done.6, bf16[256,8192]{1,0:T(8,128)(2,1)} %copy-done.7, bf16[4096,256]{1,0:T(8,128)(2,1)} %collective-permute-done.5.refs_4_), custom_call_target="tpu_custom_call" | custom-call | flops 2147483648 | bytes 11010048 | tf_op jit(solution)/shard_map/pallas_call | solution.py:36
  334.9 2.5 collective-permute-start.6
  337.4 9.4 %shard_map.142 = bf16[4,256,256]{2,1,0:T(8,128)(2,1)} custom-call(s32[8]{0:T(128)} %get-tuple-element.24.columns_ref, bf16[256,8192]{1,0:T(8,128)(2,1)} %bitcast.117, bf16[256,8192]{1,0:T(8,128)(2,1)} %copy-done.5, bf16[256,8192]{1,0:T(8,128)(2,1)} %copy-done.6, bf16[256,8192]{1,0:T(8,128)(2,1)} %copy-done.7, bf16[4096,256]{1,0:T(8,128)(2,1)} %collective-permute-done.7.refs_4_), custom_call_target="tpu_custom_call" | custom-call | flops 2147483648 | bytes 11010048 | tf_op jit(solution)/shard_map/pallas_call | solution.py:36
  347.6 9.5 %shard_map.143 = bf16[4,256,256]{2,1,0:T(8,128)(2,1)} custom-call(s32[8]{0:T(128)} %get-tuple-element.23.columns_ref, bf16[256,8192]{1,0:T(8,128)(2,1)} %bitcast.118, bf16[256,8192]{1,0:T(8,128)(2,1)} %copy-done.5, bf16[256,8192]{1,0:T(8,128)(2,1)} %copy-done.6, bf16[256,8192]{1,0:T(8,128)(2,1)} %copy-done.7, bf16[4096,256]{1,0:T(8,128)(2,1)} %pad_maximum_fusion.refs_4_), custom_call_target="tpu_custom_call" | custom-call | flops 2147483648 | bytes 11010048 | tf_op jit(solution)/shard_map/pallas_call | solution.py:36
  357.0 3.0 collective-permute-start.14
  360.9 9.3 %shard_map.144 = bf16[4,256,256]{2,1,0:T(8,128)(2,1)} custom-call(s32[8]{0:T(128)} %get-tuple-element.22.columns_ref, bf16[256,8192]{1,0:T(8,128)(2,1)} %bitcast.119, bf16[256,8192]{1,0:T(8,128)(2,1)} %copy-done.5, bf16[256,8192]{1,0:T(8,128)(2,1)} %copy-done.6, bf16[256,8192]{1,0:T(8,128)(2,1)} %copy-done.7, bf16[4096,256]{1,0:T(8,128)(2,1)} %copy-done.9), custom_call_target="tpu_custom_call" | custom-call | flops 2147483648 | bytes 11010048 | tf_op jit(solution)/shard_map/pallas_call | solution.py:36
  371.1 9.3 %shard_map.145 = bf16[4,256,256]{2,1,0:T(8,128)(2,1)} custom-call(s32[8]{0:T(128)} %get-tuple-element.27.columns_ref, bf16[256,8192]{1,0:T(8,128)(2,1)} %bitcast.120, bf16[256,8192]{1,0:T(8,128)(2,1)} %copy-done.5, bf16[256,8192]{1,0:T(8,128)(2,1)} %copy-done.6, bf16[256,8192]{1,0:T(8,128)(2,1)} %copy-done.7, bf16[4096,256]{1,0:T(8,128)(2,1)} %collective-permute-done.11.refs_4_), custom_call_target="tpu_custom_call" | custom-call | flops 2147483648 | bytes 11010048 | tf_op jit(solution)/shard_map/pallas_call | solution.py:36
  380.4 9.5 %shard_map.146 = bf16[4,256,256]{2,1,0:T(8,128)(2,1)} custom-call(s32[8]{0:T(128)} %get-tuple-element.21.columns_ref, bf16[256,8192]{1,0:T(8,128)(2,1)} %bitcast.121, bf16[256,8192]{1,0:T(8,128)(2,1)} %copy-done.5, bf16[256,8192]{1,0:T(8,128)(2,1)} %copy-done.6, bf16[256,8192]{1,0:T(8,128)(2,1)} %copy-done.7, bf16[4096,256]{1,0:T(8,128)(2,1)} %collective-permute-done.10.refs_4_), custom_call_target="tpu_custom_call" | custom-call | flops 2147483648 | bytes 11010048 | tf_op jit(solution)/shard_map/pallas_call | solution.py:36
  390.8 1.8 collective-permute-done.6
  396.3 18.8 %collective-permute-done.15 = bf16[4,256,256]{2,1,0:T(8,128)(2,1)S(1)} collective-permute-done((bf16[4,256,256]{2,1,0:T(8,128)(2,1)}, bf16[4,256,256]{2,1,0:T(8,128)(2,1)S(1)}, u32[]{:S(2)}, u32[]{:S(2)}) %collective-permute-start.15) | collective-permute-done | bytes 524320 | tf_op jit(solution)/shard_map/ppermute | solution.py:154
  415.9 12.2 %collective-permute-done.16 = bf16[4,256,256]{2,1,0:T(8,128)(2,1)S(1)} collective-permute-done((bf16[4,256,256]{2,1,0:T(8,128)(2,1)S(1)}, bf16[4,256,256]{2,1,0:T(8,128)(2,1)S(1)}, u32[]{:S(2)}, u32[]{:S(2)}) %collective-permute-start.16) | collective-permute-done | bytes 524320 | tf_op jit(solution)/shard_map/ppermute | solution.py:154
  429.8 2.9 gather_fusion.3
  433.3 1.5 copy.38
  434.8 3.7 all-to-all-start.1
  441.0 1.6 gather_fusion.4
  442.6 21.5 %all-to-all-done.1 = bf16[2,8,2,4,64,128]{5,4,2,1,0,3:T(8,128)(2,1)S(1)} async-done(((bf16[2,8,2,4,64,128]{5,4,2,1,0,3:T(8,128)(2,1)}), bf16[2,8,2,4,64,128]{5,4,2,1,0,3:T(8,128)(2,1)S(1)}, u32[]{:S(2)}, u32[]{:S(2)}) %all-to-all-start.1) | async-done | bytes 2097184 | tf_op jit(solution)/shard_map/all_to_all | solution.py:225
  464.1 1.6 copy.39
  465.7 4.2 shard_map.147
  469.8 1.7 fusion.27
  471.6 1.5 gather_fusion.6
  473.1 1.5 gather_fusion.5
  474.7 3.5 fusion.3
  478.8 3.5 all-to-all-start.2
  482.4 1.3 pad_maximum_fusion.2
  484.2 3.1 fusion.29
  491.3 3.5 all-to-all-start.3
  494.8 1.3 fusion
  496.7 1.7 shard_map.148
  498.4 5.2 %all-to-all-done.3 = bf16[2,4,64,512]{3,2,0,1:T(8,128)(2,1)S(1)} async-done(((bf16[2,4,64,512]{3,2,0,1:T(8,128)(2,1)}), bf16[2,4,64,512]{3,2,0,1:T(8,128)(2,1)S(1)}, u32[]{:S(2)}, u32[]{:S(2)}) %all-to-all-start.3) | async-done | bytes 524320 | tf_op jit(solution)/shard_map/all_to_all | solution.py:264
  (119 shorter events, 29.7 us)
Async XLA Ops:
  7.2 233.3 %copy-start = (s32[32]{0:T(128)S(1)}, s32[32]{0:T(128)}, u32[]{:S(2)}) copy-start(s32[32]{0:T(128)} %param.12) | copy-start | bytes 388
  7.2 467.5 %all-gather.3.cloned.1.call-start = ((), (), s32[]{:S(2)}) async-start(), calls=%async_computation.4 | async-start | bytes 5242880 | tf_op jit(solution)/shard_map/all_gather | solution.py:191
  16.1 127.4 %copy-start.19 = (s32[8,8]{1,0:T(8,128)S(1)}, s32[8,8]{1,0:T(8,128)}, u32[]{:S(2)}) copy-start(s32[8,8]{1,0:T(8,128)} %param.13) | copy-start | bytes 772
  46.2 2.9 copy-start.4
  46.3 103.9 %copy-start.8 = (bf16[8,2,4,64,256]{4,3,2,1,0:T(8,128)(2,1)}, bf16[8,2,4,64,256]{4,3,2,1,0:T(8,128)(2,1)S(1)}, u32[]{:S(2)}) copy-start(bf16[8,2,4,64,256]{4,3,2,1,0:T(8,128)(2,1)S(1)} %copy.37) | copy-start | bytes 6291460
  49.1 91.9 %collective-permute-start = (bf16[256,8192]{1,0:T(8,128)(2,1)S(1)}, bf16[256,8192]{1,0:T(8,128)(2,1)S(1)}, u32[]{:S(2)}, u32[]{:S(2)}) collective-permute-start(bf16[256,8192]{1,0:T(8,128)(2,1)S(1)} %bitcast.122), channel_id=1, source_target_pairs={{0,2},{1,3},{2,0},{3,1},{4,6},{5,7},{6,4},{7,5},{8,10},{9,11},{10,... | collective-permute-start | bytes 12582920 | tf_op jit(solution)/shard_map/ppermute | solution.py:175
  49.5 94.5 %collective-permute-start.1 = (bf16[256,8192]{1,0:T(8,128)(2,1)S(1)}, bf16[256,8192]{1,0:T(8,128)(2,1)S(1)}, u32[]{:S(2)}, u32[]{:S(2)}) collective-permute-start(bf16[256,8192]{1,0:T(8,128)(2,1)S(1)} %bitcast.123), channel_id=1, source_target_pairs={{0,1},{1,0},{2,3},{3,2},{4,5},{5,4},{6,7},{7,6},{8,9},{9,8},{10,11... | collective-permute-start | bytes 12582920 | tf_op jit(solution)/shard_map/ppermute | solution.py:175
  141.1 7.2 %copy-start.5 = (bf16[256,8192]{1,0:T(8,128)(2,1)}, bf16[256,8192]{1,0:T(8,128)(2,1)S(1)}, u32[]{:S(2)}) copy-start(bf16[256,8192]{1,0:T(8,128)(2,1)S(1)} %collective-permute-done.refs_1_) | copy-start | bytes 12582916
  141.1 7.2 %collective-permute-start.2 = (bf16[256,8192]{1,0:T(8,128)(2,1)S(1)}, bf16[256,8192]{1,0:T(8,128)(2,1)S(1)}, u32[]{:S(2)}, u32[]{:S(2)}) collective-permute-start(bf16[256,8192]{1,0:T(8,128)(2,1)S(1)} %collective-permute-done.refs_1_), channel_id=1, source_target_pairs={{0,1},{1,0},{2,3},{3,2},{4,5},{5,4},{6,7},{7,6},{8,9},{9,8},{10,11... | collective-permute-start | bytes 12582920 | tf_op jit(solution)/shard_map/ppermute | solution.py:175
  141.1 48.8 %collective-permute-start.10 = (bf16[4096,256]{1,0:T(8,128)(2,1)S(1)}, bf16[4096,256]{1,0:T(8,128)(2,1)}, u32[]{:S(2)}, u32[]{:S(2)}) collective-permute-start(bf16[4096,256]{1,0:T(8,128)(2,1)S(1)} %bitcast.129), channel_id=1, source_target_pairs={{0,4},{8,0},{16,8},{24,16},{28,24},{20,28},{12,20},{4,12},{1,5},{9... | collective-permute-start | bytes 6291464 | tf_op jit(solution)/shard_map/ppermute | solution.py:154
  143.4 48.1 %collective-permute-start.3 = (bf16[4096,256]{1,0:T(8,128)(2,1)S(1)}, bf16[4096,256]{1,0:T(8,128)(2,1)}, u32[]{:S(2)}, u32[]{:S(2)}) collective-permute-start(bf16[4096,256]{1,0:T(8,128)(2,1)S(1)} %bitcast.130), channel_id=1, source_target_pairs={{0,8},{8,16},{16,24},{24,28},{28,20},{20,12},{12,4},{4,0},{1,9},{9... | collective-permute-start | bytes 6291464 | tf_op jit(solution)/shard_map/ppermute | solution.py:154
  144.0 4.2 copy-start.6
  148.2 2.0 copy-start.7
  150.2 89.5 %copy-start.2 = (s32[8]{0:T(128)S(1)}, s32[8]{0:T(128)}, u32[]{:S(2)}) copy-start(s32[8]{0:T(128)} %constant.125.clone) | copy-start | bytes 100
  159.7 324.5 %all-gather.5.cloned.1.call-start = ((), (), s32[]{:S(2)}) async-start(), calls=%async_computation.5 | async-start | bytes 5242880 | tf_op jit(solution)/shard_map/all_gather | solution.py:192
  189.9 47.8 %collective-permute-start.11 = (bf16[4096,256]{1,0:T(8,128)(2,1)}, bf16[4096,256]{1,0:T(8,128)(2,1)}, u32[]{:S(2)}, u32[]{:S(2)}) collective-permute-start(bf16[4096,256]{1,0:T(8,128)(2,1)} %collective-permute-done.10.refs_4_), channel_id=1, source_target_pairs={{0,4},{8,0},{16,8},{24,16},{28,24},{20,28},{12,20},{4,12},{1,5},{9... | collective-permute-start | bytes 6291464 | tf_op jit(solution)/shard_map/ppermute | solution.py:154
  191.6 47.5 %collective-permute-start.5 = (bf16[4096,256]{1,0:T(8,128)(2,1)}, bf16[4096,256]{1,0:T(8,128)(2,1)}, u32[]{:S(2)}, u32[]{:S(2)}) collective-permute-start(bf16[4096,256]{1,0:T(8,128)(2,1)} %collective-permute-done.3.refs_4_), channel_id=1, source_target_pairs={{0,8},{8,16},{16,24},{24,28},{28,20},{20,12},{12,4},{4,0},{1,9},{9... | collective-permute-start | bytes 6291464 | tf_op jit(solution)/shard_map/ppermute | solution.py:154
  237.7 46.8 %collective-permute-start.12 = (bf16[4096,256]{1,0:T(8,128)(2,1)}, bf16[4096,256]{1,0:T(8,128)(2,1)S(1)}, u32[]{:S(2)}, u32[]{:S(2)}) collective-permute-start(bf16[4096,256]{1,0:T(8,128)(2,1)} %collective-permute-done.11.refs_4_), channel_id=1, source_target_pairs={{0,4},{8,0},{16,8},{24,16},{28,24},{20,28},{12,20},{4,12},{1,5},{9... | collective-permute-start | bytes 6291464 | tf_op jit(solution)/shard_map/ppermute | solution.py:154
  239.1 46.7 %collective-permute-start.7 = (bf16[4096,256]{1,0:T(8,128)(2,1)}, bf16[4096,256]{1,0:T(8,128)(2,1)}, u32[]{:S(2)}, u32[]{:S(2)}) collective-permute-start(bf16[4096,256]{1,0:T(8,128)(2,1)} %collective-permute-done.5.refs_4_), channel_id=1, source_target_pairs={{0,8},{8,16},{16,24},{24,28},{28,20},{20,12},{12,4},{4,0},{1,9},{9... | collective-permute-start | bytes 6291464 | tf_op jit(solution)/shard_map/ppermute | solution.py:154
  242.6 50.9 %copy-start.18 = (s32[8]{0:T(128)S(1)}, s32[8]{0:T(128)}, u32[]{:S(2)}) copy-start(s32[8]{0:T(128)} %constant.124.clone) | copy-start | bytes 100
  242.6 61.1 %copy-start.3 = (s32[4]{0:T(128)S(1)}, s32[4]{0:T(128)}, u32[]{:S(2)}) copy-start(s32[4]{0:T(128)} %constant.126.clone) | copy-start | bytes 52
  284.5 3.5 copy-start.9
  284.5 25.3 %collective-permute-start.13 = (bf16[2048,256]{1,0:T(8,128)(2,1)S(1)}, bf16[2048,256]{1,0:T(8,128)(2,1)}, u32[]{:S(2)}, u32[]{:S(2)}) collective-permute-start(bf16[2048,256]{1,0:T(8,128)(2,1)S(1)} %slice.52), channel_id=1, source_target_pairs={{0,4},{8,0},{16,8},{24,16},{28,24},{20,28},{12,20},{4,12},{1,5},{9... | collective-permute-start | bytes 3145736 | tf_op jit(solution)/shard_map/ppermute | solution.py:154
  288.0 23.2 %collective-permute-start.9 = (bf16[2048,256]{1,0:T(8,128)(2,1)}, bf16[2048,256]{1,0:T(8,128)(2,1)}, u32[]{:S(2)}, u32[]{:S(2)}) collective-permute-start(bf16[2048,256]{1,0:T(8,128)(2,1)} %slice.51), channel_id=1, source_target_pairs={{0,8},{8,16},{16,24},{24,28},{28,20},{20,12},{12,4},{4,0},{1,9},{9... | collective-permute-start | bytes 3145736 | tf_op jit(solution)/shard_map/ppermute | solution.py:154
  323.8 66.0 %collective-permute-start.4 = (bf16[4,256,256]{2,1,0:T(8,128)(2,1)}, bf16[4,256,256]{2,1,0:T(8,128)(2,1)S(1)}, u32[]{:S(2)}, u32[]{:S(2)}) collective-permute-start(bf16[4,256,256]{2,1,0:T(8,128)(2,1)} %shard_map.140), channel_id=1, source_target_pairs={{0,4},{8,0},{16,8},{24,16},{28,24},{20,28},{12,20},{4,12},{1,5},{9... | collective-permute-start | bytes 1572872 | tf_op jit(solution)/shard_map/ppermute | solution.py:154
  334.9 57.8 %collective-permute-start.6 = (bf16[4,256,256]{2,1,0:T(8,128)(2,1)}, bf16[4,256,256]{2,1,0:T(8,128)(2,1)S(1)}, u32[]{:S(2)}, u32[]{:S(2)}) collective-permute-start(bf16[4,256,256]{2,1,0:T(8,128)(2,1)} %shard_map.141), channel_id=1, source_target_pairs={{0,12},{8,4},{16,0},{24,8},{28,16},{20,24},{12,28},{4,20},{1,13},{... | collective-permute-start | bytes 1572872 | tf_op jit(solution)/shard_map/ppermute | solution.py:154
  346.8 47.8 %collective-permute-start.8 = (bf16[4,256,256]{2,1,0:T(8,128)(2,1)}, bf16[4,256,256]{2,1,0:T(8,128)(2,1)S(1)}, u32[]{:S(2)}, u32[]{:S(2)}) collective-permute-start(bf16[4,256,256]{2,1,0:T(8,128)(2,1)} %shard_map.142), channel_id=1, source_target_pairs={{0,20},{8,12},{16,4},{24,0},{28,8},{20,16},{12,24},{4,28},{1,21},{... | collective-permute-start | bytes 1572872 | tf_op jit(solution)/shard_map/ppermute | solution.py:154
  347.5 12.5 %copy-start.14 = (bf16[4,256,256]{2,1,0:T(8,128)(2,1)S(1)}, bf16[4,256,256]{2,1,0:T(8,128)(2,1)}, u32[]{:S(2)}) copy-start(bf16[4,256,256]{2,1,0:T(8,128)(2,1)} %shard_map.139) | copy-start | bytes 1572868
  357.0 38.4 %collective-permute-start.14 = (bf16[4,256,256]{2,1,0:T(8,128)(2,1)}, bf16[4,256,256]{2,1,0:T(8,128)(2,1)S(1)}, u32[]{:S(2)}, u32[]{:S(2)}) collective-permute-start(bf16[4,256,256]{2,1,0:T(8,128)(2,1)} %shard_map.143), channel_id=1, source_target_pairs={{0,28},{8,20},{16,12},{24,4},{28,0},{20,8},{12,16},{4,24},{1,29},{... | collective-permute-start | bytes 1572872 | tf_op jit(solution)/shard_map/ppermute | solution.py:154
  370.2 44.9 %collective-permute-start.15 = (bf16[4,256,256]{2,1,0:T(8,128)(2,1)}, bf16[4,256,256]{2,1,0:T(8,128)(2,1)S(1)}, u32[]{:S(2)}, u32[]{:S(2)}) collective-permute-start(bf16[4,256,256]{2,1,0:T(8,128)(2,1)} %shard_map.144), channel_id=1, source_target_pairs={{0,24},{8,28},{16,20},{24,12},{28,4},{20,0},{12,8},{4,16},{1,25},{... | collective-permute-start | bytes 1572872 | tf_op jit(solution)/shard_map/ppermute | solution.py:154
  380.4 9.5 %copy-start.15 = (bf16[4,256,256]{2,1,0:T(8,128)(2,1)S(1)}, bf16[4,256,256]{2,1,0:T(8,128)(2,1)}, u32[]{:S(2)}) copy-start(bf16[4,256,256]{2,1,0:T(8,128)(2,1)} %shard_map.145) | copy-start | bytes 1572868
  389.9 38.2 %collective-permute-start.16 = (bf16[4,256,256]{2,1,0:T(8,128)(2,1)S(1)}, bf16[4,256,256]{2,1,0:T(8,128)(2,1)S(1)}, u32[]{:S(2)}, u32[]{:S(2)}) collective-permute-start(bf16[4,256,256]{2,1,0:T(8,128)(2,1)S(1)} %copy-done.15), channel_id=1, source_target_pairs={{0,16},{8,24},{16,28},{24,20},{28,12},{20,4},{12,0},{4,8},{1,17},{... | collective-permute-start | bytes 1572872 | tf_op jit(solution)/shard_map/ppermute | solution.py:154
  392.6 36.3 %collective-permute-start.17 = (bf16[4,256,256]{2,1,0:T(8,128)(2,1)}, bf16[4,256,256]{2,1,0:T(8,128)(2,1)S(1)}, u32[]{:S(2)}, u32[]{:S(2)}) collective-permute-start(bf16[4,256,256]{2,1,0:T(8,128)(2,1)} %shard_map.146), channel_id=1, source_target_pairs={{0,8},{8,16},{16,24},{24,28},{28,20},{20,12},{12,4},{4,0},{1,9},{9... | collective-permute-start | bytes 1572872 | tf_op jit(solution)/shard_map/ppermute | solution.py:154
  434.8 3.8 copy-start.16
  434.8 29.4 %all-to-all-start.1 = ((bf16[2,8,2,4,64,128]{5,4,2,1,0,3:T(8,128)(2,1)}), bf16[2,8,2,4,64,128]{5,4,2,1,0,3:T(8,128)(2,1)S(1)}, u32[]{:S(2)}, u32[]{:S(2)}) async-start(bf16[2,8,2,4,64,128]{5,4,2,1,0,3:T(8,128)(2,1)} %copy.38), calls=%async_computation.1 | async-start | bytes 4194304 | tf_op jit(solution)/shard_map/all_to_all | solution.py:225
  471.6 6.6 %copy-start.11 = (bf16[16,64,512]{2,1,0:T(8,128)(2,1)}, bf16[16,64,512]{2,1,0:T(8,128)(2,1)S(1)}, u32[]{:S(2)}) copy-start(bf16[16,64,512]{2,1,0:T(8,128)(2,1)S(1)} %get-tuple-element.17) | copy-start | bytes 3145732
  478.8 12.4 %all-to-all-start.2 = ((bf16[2,4,64,128]{3,2,0,1:T(8,128)(2,1)}), bf16[2,4,64,128]{3,2,0,1:T(8,128)(2,1)S(1)}, u32[]{:S(2)}, u32[]{:S(2)}) async-start(bf16[2,4,64,128]{3,2,0,1:T(8,128)(2,1)} %copy.41), calls=%async_computation.2 | async-start | bytes 262144 | tf_op jit(solution)/shard_map/all_to_all | solution.py:225
  484.2 4.2 copy-start.12
  484.2 4.2 copy-start.13
  488.4 1.2 copy-start.10
  491.3 12.3 %all-to-all-start.3 = ((bf16[2,4,64,512]{3,2,0,1:T(8,128)(2,1)}), bf16[2,4,64,512]{3,2,0,1:T(8,128)(2,1)S(1)}, u32[]{:S(2)}, u32[]{:S(2)}) async-start(bf16[2,4,64,512]{3,2,0,1:T(8,128)(2,1)} %copy.44), calls=%async_computation.3 | async-start | bytes 1048576 | tf_op jit(solution)/shard_map/all_to_all | solution.py:264
  494.7 9.6 %copy-start.1 = (s32[32]{0:T(128)S(1)}, s32[32]{0:T(128)}, u32[]{:S(2)}) copy-start(s32[32]{0:T(128)} %param.12) | copy-start | bytes 388
  494.8 8.8 %copy-start.17 = (bf16[1,2,64,512]{3,2,1,0:T(8,128)(2,1)S(1)}, bf16[1,2,64,512]{3,2,1,0:T(8,128)(2,1)}, u32[]{:S(2)}) copy-start(bf16[1,2,64,512]{3,2,1,0:T(8,128)(2,1)} %param.18) | copy-start | bytes 393220
Sparse Core Ops, SparseCore 0:
  159.8 35.8 all-gather.2
  310.0 34.6 all-gather.4

commit v2 on v1

--- a/solution.py
+++ b/solution.py
@@ -177,6 +177,18 @@
         offsets = offsets + [offset ^ bit for offset in offsets]
         bit //= 2
 
+    strip_slot = {offset: j for j, offset in enumerate(offsets)}
+    slot_array = jnp.array([strip_slot[offset] for offset in range(procs)], jnp.int32)
+    slots = slot_array[jnp.arange(procs, dtype=jnp.int32) ^ proc_index]
+
+    def gather_rows(panel_rows):
+        parts, bit = [panel_rows], procs // 2
+        while bit:
+            pairs = [(q, q ^ bit) for q in range(procs)]
+            parts = parts + [lax.ppermute(part, "proc", pairs) for part in parts]
+            bit //= 2
+        return jnp.moveaxis(jnp.stack(parts)[slots], 0, 2).reshape(-1, width)
+
     def send_home(arrived, distance):
         columns = structure[order_array[(place - distance) % groups]]
         product = structured_product(columns, strips, arrived)
@@ -188,8 +200,7 @@
         (received[0], (local_parent, local_child))
     )
     local_parent, local_child = panels_after
-    whole_parent = lax.all_gather(local_parent, "proc", axis=2, tiled=True).reshape(-1, width)
-    whole_child = lax.all_gather(local_child, "proc", axis=2, tiled=True).reshape(-1, width)
+    whole_parent, whole_child = gather_rows(local_parent), gather_rows(local_child)
     forth = back = panel
     half = panel.shape[0] // 2
     for distance in range(1, groups // 2):
@@ -210,9 +221,6 @@
     slab_index = piece_owner[wanted]
     ahead = (place_array[slab_index // owned_count] - place) % groups
     within = slab_index % owned_count
-    strip_slot = {offset: j for j, offset in enumerate(offsets)}
-    slot_array = jnp.array([strip_slot[offset] for offset in range(procs)], jnp.int32)
-    slots = slot_array[jnp.arange(procs, dtype=jnp.int32) ^ proc_index]
     index = (ahead[:, :, None] * procs + slots[None, None, :]) * owned_count + within[:, :, None]
     products = gathered[index.reshape(-1)].reshape(
         blocks, pieces, procs, strip_rows, 2 * slice_width

time: 519 us -> 434 us (0.84)
  waiting for transfers between devices: 274 us -> 158 us
  starting transfers between devices: 29.9 us -> 47.5 us
  local copies, waits for them, and re-layouts: 36.9 us -> 53.4 us
  between operations: 33 us -> 19.3 us
  other arithmetic: 10.9 us -> 18.4 us
    ppermute x3, waiting for transfers between devices: 95.8 us -> 41 us  [per_device(): arrived.append(lax.ppermute(strip, 'proc', pairs))]
    ppermute x15, waiting for transfers between devices: 152 us -> 112 us  [shift(): return lax.ppermute(value, 'group', pairs)]
    all_to_all x2, waiting for transfers between devices: 21.5 us -> 0.01 us  [to_strips(): lax.all_to_all(value, 'proc', split_axis=len(lead), concat_axis=len(lead)...]
    ppermute x15, starting transfers between devices: 18.7 us -> 33.4 us  [shift(): return lax.ppermute(value, 'group', pairs)]
    gather x0 -> x2, local copies, waits for them, and re-layouts: none -> 10.1 us  [gather_rows(): return jnp.moveaxis(jnp.stack(parts)[slots], 0, 2).reshape(-1, width)]
    another operation x0 -> x2, other arithmetic: none -> 7.44 us  [gather_rows(): return jnp.moveaxis(jnp.stack(parts)[slots], 0, 2).reshape(-1, width)]
    unnamed x47 -> x49, local copies, waits for them, and re-layouts: 11.3 us -> 9.16 us
  transfers between devices with their start and end apart: 23 -> 27, of which waited for: 11 -> 8; matrix products, arithmetic and copies ran while one was open for 9% -> 18% of each run, Pallas kernels for 16% -> 15%
where the time goes in v2:
time: 434 us; the launch traced here: 426 us
  waiting for transfers between devices  158 us (36%)
  Pallas kernels  87.4 us (20%)
  local copies, waits for them, and re-layouts  53.4 us (12%)
  starting transfers between devices  47.5 us (11%)
  blocking collectives  30 us (7%)
  between operations  19.3 us (4%)
  other arithmetic  18.4 us (4%)
  matrix products  11.8 us (3%)
    ppermute x15, waiting for transfers between devices, shift(): return lax.ppermute(value, 'group', pairs)  112 us
    pallas_call x8, Pallas kernels, structured_product(): pl.pallas_call(functools.partial(product_kernel, count), out_shape=jax.Sh...  74.7 us
    ppermute x3, waiting for transfers between devices, per_device(): arrived.append(lax.ppermute(strip, 'proc', pairs))  41 us
    ppermute x15, starting transfers between devices, shift(): return lax.ppermute(value, 'group', pairs)  33.4 us
    all_to_all x1, blocking collectives, per_device(): lax.all_to_all(packed, 'proc', split_axis=0, concat_axis=0, tiled=True)  30 us
    gather x2, local copies, waits for them, and re-layouts, gather_rows(): return jnp.moveaxis(jnp.stack(parts)[slots], 0, 2).reshape(-1, width)  10.1 us
    unnamed x49, local copies, waits for them, and re-layouts  9.16 us
  transfers between devices with their start and end apart: 27, of which 8 were waited for; matrix products, arithmetic and copies ran while one was open for 18% of the time, Pallas kernels for 15%

profile of v2, /device:TPU:0, one launch (start us, length us, event | category | flops | bytes accessed | tf_op | source)
XLA Modules:
  0.0 425.5 jit_solution(12679366791797774100)
XLA Ops:
  2.6 6.9 %shard_map.138 = bf16[4,8,2,64,256]{4,3,2,1,0:T(8,128)(2,1)} custom-call(s32[8]{0:T(128)} %select_reduce_fusion.source_ref, s32[8]{0:T(128)} %convert_element_type.45.met_ref, bf16[8,2,64,512]{3,2,1,0:T(8,128)(2,1)} %bitcast.148, bf16[8,2,64,512]{3,2,1,0:T(8,128)(2,1)} %bitcast.3.child_ref), custom_call_target="tpu_custom_call" | custom-call | tf_op jit(solution)/shard_map/pallas_call | solution.py:78
  9.5 30.0 %all_to_all.20 = bf16[4,8,2,64,256]{4,3,2,1,0:T(8,128)(2,1)S(1)} all-to-all(bf16[4,8,2,64,256]{4,3,2,1,0:T(8,128)(2,1)} %shard_map.138), channel_id=1, replica_groups=mesh['group'=8,'proc'=4] {'proc'}, dimensions={0} | all-to-all | bytes 4194304 | tf_op jit(solution)/shard_map/all_to_all | solution.py:164
  40.2 2.3 collective-permute-start.10
  42.6 45.4 %collective-permute-done.10.refs_4_ = bf16[4096,256]{1,0:T(8,128)(2,1)S(1)} collective-permute-done((bf16[4096,256]{1,0:T(8,128)(2,1)S(1)}, bf16[4096,256]{1,0:T(8,128)(2,1)S(1)}, u32[]{:S(2)}, u32[]{:S(2)}) %collective-permute-start.10) | collective-permute-done | bytes 2097184 | tf_op jit(solution)/shard_map/ppermute | solution.py:154
  88.0 1.7 collective-permute-start.11
  91.1 41.0 %collective-permute-done.refs_1_ = bf16[256,8192]{1,0:T(8,128)(2,1)} collective-permute-done((bf16[256,8192]{1,0:T(8,128)(2,1)}, bf16[256,8192]{1,0:T(8,128)(2,1)}, u32[]{:S(2)}, u32[]{:S(2)}) %collective-permute-start) | collective-permute-done | bytes 4194336 | tf_op jit(solution)/shard_map/ppermute | solution.py:175
  132.1 2.7 collective-permute-done.11.refs_4_
  142.6 38.5 %collective-permute-done.12.refs_4_ = bf16[4096,256]{1,0:T(8,128)(2,1)} collective-permute-done((bf16[4096,256]{1,0:T(8,128)(2,1)}, bf16[4096,256]{1,0:T(8,128)(2,1)}, u32[]{:S(2)}, u32[]{:S(2)}) %collective-permute-start.12) | collective-permute-done | bytes 2097184 | tf_op jit(solution)/shard_map/ppermute | solution.py:154
  182.4 1.7 collective-permute-start.13
  206.6 1.7 collective-permute-done.9
  208.2 2.7 pad_maximum_fusion.2.refs_4_
  210.9 9.3 %shard_map.139 = bf16[4,256,256]{2,1,0:T(8,128)(2,1)} custom-call(s32[8]{0:T(128)} %get-tuple-element.15.columns_ref, bf16[256,8192]{1,0:T(8,128)(2,1)} %bitcast.6.refs_0_, bf16[256,8192]{1,0:T(8,128)(2,1)} %collective-permute-done.refs_1_, bf16[256,8192]{1,0:T(8,128)(2,1)} %collective-permute-done.1.refs_2_, ...), custom_call_target="tpu_custom_call" | custom-call | flops 2147483648 | bytes 11010048 | tf_op jit(solution)/shard_map/pallas_call | solution.py:36
  220.2 1.9 bitcast_dynamic-update-slice_fusion.7
  222.1 9.3 %shard_map.140 = bf16[4,256,256]{2,1,0:T(8,128)(2,1)} custom-call(s32[8]{0:T(128)} %get-tuple-element.26.columns_ref, bf16[256,8192]{1,0:T(8,128)(2,1)} %bitcast.6.refs_0_, bf16[256,8192]{1,0:T(8,128)(2,1)} %collective-permute-done.refs_1_, bf16[256,8192]{1,0:T(8,128)(2,1)} %collective-permute-done.1.refs_2_, ...), custom_call_target="tpu_custom_call" | custom-call | flops 2147483648 | bytes 11010048 | tf_op jit(solution)/shard_map/pallas_call | solution.py:36
  233.0 9.3 %shard_map.141 = bf16[4,256,256]{2,1,0:T(8,128)(2,1)} custom-call(s32[8]{0:T(128)} %get-tuple-element.25.columns_ref, bf16[256,8192]{1,0:T(8,128)(2,1)} %bitcast.6.refs_0_, bf16[256,8192]{1,0:T(8,128)(2,1)} %collective-permute-done.refs_1_, bf16[256,8192]{1,0:T(8,128)(2,1)} %collective-permute-done.1.refs_2_, ...), custom_call_target="tpu_custom_call" | custom-call | flops 2147483648 | bytes 11010048 | tf_op jit(solution)/shard_map/pallas_call | solution.py:36
  242.3 2.6 collective-permute-start.6
  244.8 9.4 %shard_map.142 = bf16[4,256,256]{2,1,0:T(8,128)(2,1)} custom-call(s32[8]{0:T(128)} %get-tuple-element.24.columns_ref, bf16[256,8192]{1,0:T(8,128)(2,1)} %bitcast.6.refs_0_, bf16[256,8192]{1,0:T(8,128)(2,1)} %collective-permute-done.refs_1_, bf16[256,8192]{1,0:T(8,128)(2,1)} %collective-permute-done.1.refs_2_, ...), custom_call_target="tpu_custom_call" | custom-call | flops 2147483648 | bytes 11010048 | tf_op jit(solution)/shard_map/pallas_call | solution.py:36
  254.5 9.4 %shard_map.143 = bf16[4,256,256]{2,1,0:T(8,128)(2,1)} custom-call(s32[8]{0:T(128)} %get-tuple-element.23.columns_ref, bf16[256,8192]{1,0:T(8,128)(2,1)} %bitcast.6.refs_0_, bf16[256,8192]{1,0:T(8,128)(2,1)} %collective-permute-done.refs_1_, bf16[256,8192]{1,0:T(8,128)(2,1)} %collective-permute-done.1.refs_2_, ...), custom_call_target="tpu_custom_call" | custom-call | flops 2147483648 | bytes 11010048 | tf_op jit(solution)/shard_map/pallas_call | solution.py:36
  263.8 3.4 collective-permute-start.14
  268.1 9.3 %shard_map.144 = bf16[4,256,256]{2,1,0:T(8,128)(2,1)} custom-call(s32[8]{0:T(128)} %get-tuple-element.22.columns_ref, bf16[256,8192]{1,0:T(8,128)(2,1)} %bitcast.6.refs_0_, bf16[256,8192]{1,0:T(8,128)(2,1)} %collective-permute-done.refs_1_, bf16[256,8192]{1,0:T(8,128)(2,1)} %collective-permute-done.1.refs_2_, ...), custom_call_target="tpu_custom_call" | custom-call | flops 2147483648 | bytes 11010048 | tf_op jit(solution)/shard_map/pallas_call | solution.py:36
  277.4 9.3 %shard_map.145 = bf16[4,256,256]{2,1,0:T(8,128)(2,1)} custom-call(s32[8]{0:T(128)} %get-tuple-element.27.columns_ref, bf16[256,8192]{1,0:T(8,128)(2,1)} %bitcast.6.refs_0_, bf16[256,8192]{1,0:T(8,128)(2,1)} %collective-permute-done.refs_1_, bf16[256,8192]{1,0:T(8,128)(2,1)} %collective-permute-done.1.refs_2_, ...), custom_call_target="tpu_custom_call" | custom-call | flops 2147483648 | bytes 11010048 | tf_op jit(solution)/shard_map/pallas_call | solution.py:36
  286.8 9.5 %shard_map.146 = bf16[4,256,256]{2,1,0:T(8,128)(2,1)} custom-call(s32[8]{0:T(128)} %get-tuple-element.21.columns_ref, bf16[256,8192]{1,0:T(8,128)(2,1)} %bitcast.6.refs_0_, bf16[256,8192]{1,0:T(8,128)(2,1)} %collective-permute-done.refs_1_, bf16[256,8192]{1,0:T(8,128)(2,1)} %collective-permute-done.1.refs_2_, ...), custom_call_target="tpu_custom_call" | custom-call | flops 2147483648 | bytes 11010048 | tf_op jit(solution)/shard_map/pallas_call | solution.py:36
  296.4 1.9 bitcast_dynamic-update-slice_fusion.6
  299.5 1.9 bitcast_dynamic-update-slice_fusion.5
  301.4 9.1 %collective-permute-start.16 = (bf16[4,256,256]{2,1,0:T(8,128)(2,1)S(1)}, bf16[4,256,256]{2,1,0:T(8,128)(2,1)S(1)}, u32[]{:S(2)}, u32[]{:S(2)}) collective-permute-start(bf16[4,256,256]{2,1,0:T(8,128)(2,1)S(1)} %copy-done.14), channel_id=1, source_target_pairs={{0,16},{8,24},{16,28},{24,20},{28,12},{20,4},{12,0},{4,8},{1,17},{... | collective-permute-start | bytes 1572872 | tf_op jit(solution)/shard_map/ppermute | solution.py:154
  311.3 5.8 %collective-permute-start.17 = (bf16[4,256,256]{2,1,0:T(8,128)(2,1)}, bf16[4,256,256]{2,1,0:T(8,128)(2,1)S(1)}, u32[]{:S(2)}, u32[]{:S(2)}) collective-permute-start(bf16[4,256,256]{2,1,0:T(8,128)(2,1)} %shard_map.146), channel_id=1, source_target_pairs={{0,8},{8,16},{16,24},{24,28},{28,20},{20,12},{12,4},{4,0},{1,9},{9... | collective-permute-start | bytes 1572872 | tf_op jit(solution)/shard_map/ppermute | solution.py:154
  318.0 13.0 %collective-permute-done.15 = bf16[4,256,256]{2,1,0:T(8,128)(2,1)S(1)} collective-permute-done((bf16[4,256,256]{2,1,0:T(8,128)(2,1)S(1)}, bf16[4,256,256]{2,1,0:T(8,128)(2,1)S(1)}, u32[]{:S(2)}, u32[]{:S(2)}) %collective-permute-start.15) | collective-permute-done | bytes 524320 | tf_op jit(solution)/shard_map/ppermute | solution.py:154
  332.4 10.4 %collective-permute-done.16 = bf16[4,256,256]{2,1,0:T(8,128)(2,1)S(1)} collective-permute-done((bf16[4,256,256]{2,1,0:T(8,128)(2,1)S(1)}, bf16[4,256,256]{2,1,0:T(8,128)(2,1)S(1)}, u32[]{:S(2)}, u32[]{:S(2)}) %collective-permute-start.16) | collective-permute-done | bytes 524320 | tf_op jit(solution)/shard_map/ppermute | solution.py:154
  344.9 2.9 gather_fusion.3
  347.8 1.6 slice_negate_fusion
  351.1 3.8 all-to-all-start.1
  354.9 2.8 gather_fusion.5
  357.7 3.8 pad_maximum_fusion.1
  361.5 5.0 %gather_fusion.6 = bf16[4,8,2,64,512]{4,3,2,1,0:T(8,128)(2,1)} fusion(bf16[4,8,2,64,512]{4,3,2,1,0:T(8,128)(2,1)} %pad_maximum_fusion.1, s32[1024]{0:T(1024)S(1)} %pad_clamp_fusion.1), kind=kCustom, calls=%fused_computation.6 | custom fusion | bytes 8388624 | tf_op jit(solution)/shard_map/gather | solution.py:190
  366.6 1.9 slice.60
  368.4 4.6 %copy.44 = bf16[8,2,4,64,512]{4,3,2,1,0:T(8,128)(2,1)} copy(bf16[8,2,4,64,512]{4,3,1,0,2:T(8,128)(2,1)} %bitcast.137) | data formatting | bytes 8388608 | tf_op jit(solution)/shard_map/transpose | solution.py:190
  373.1 3.6 pad_maximum_fusion
  376.7 5.1 %gather_fusion.4 = bf16[4,8,2,64,512]{4,3,2,1,0:T(8,128)(2,1)} fusion(bf16[4,8,2,64,512]{4,3,2,1,0:T(8,128)(2,1)} %pad_maximum_fusion, s32[1024]{0:T(1024)S(1)} %pad_clamp_fusion.1), kind=kCustom, calls=%fused_computation.4 | custom fusion | bytes 8388624 | tf_op jit(solution)/shard_map/gather | solution.py:190
  381.8 3.9 fusion.11
  389.8 3.7 fusion.40
  393.5 3.3 all-to-all-start.2
  398.4 4.1 shard_map.147
  402.5 1.8 fusion.38
  407.4 2.1 convert_add_fusion
  409.5 2.1 fusion.4
  412.5 3.5 all-to-all-start.3
  417.9 1.7 shard_map.148
  419.6 5.2 %all-to-all-done.3 = bf16[2,4,64,512]{3,2,0,1:T(8,128)(2,1)S(1)} async-done(((bf16[2,4,64,512]{3,2,0,1:T(8,128)(2,1)}), bf16[2,4,64,512]{3,2,0,1:T(8,128)(2,1)S(1)}, u32[]{:S(2)}, u32[]{:S(2)}) %all-to-all-start.3) | async-done | bytes 524320 | tf_op jit(solution)/shard_map/all_to_all | solution.py:272
  (134 shorter events, 40.6 us)
Async XLA Ops:
  0.6 137.6 %copy-start = (s32[32]{0:T(128)S(1)}, s32[32]{0:T(128)}, u32[]{:S(2)}) copy-start(s32[32]{0:T(128)} %param.12) | copy-start | bytes 388
  9.5 128.0 %copy-start.20 = (s32[8,8]{1,0:T(8,128)S(1)}, s32[8,8]{1,0:T(8,128)}, u32[]{:S(2)}) copy-start(s32[8,8]{1,0:T(8,128)} %param.13) | copy-start | bytes 772
  39.6 99.5 %copy-start.2 = (s32[8]{0:T(128)S(1)}, s32[8]{0:T(128)}, u32[]{:S(2)}) copy-start(s32[8]{0:T(128)} %constant.125.clone) | copy-start | bytes 100
  39.7 100.7 %copy-start.5 = (bf16[8,2,4,64,256]{4,3,2,1,0:T(8,128)(2,1)}, bf16[8,2,4,64,256]{4,3,2,1,0:T(8,128)(2,1)S(1)}, u32[]{:S(2)}) copy-start(bf16[8,2,4,64,256]{4,3,2,1,0:T(8,128)(2,1)S(1)} %copy.36) | copy-start | bytes 6291460
  39.7 92.3 %collective-permute-start = (bf16[256,8192]{1,0:T(8,128)(2,1)}, bf16[256,8192]{1,0:T(8,128)(2,1)}, u32[]{:S(2)}, u32[]{:S(2)}) collective-permute-start(bf16[256,8192]{1,0:T(8,128)(2,1)} %bitcast.6.refs_0_), channel_id=1, source_target_pairs={{0,2},{1,3},{2,0},{3,1},{4,6},{5,7},{6,4},{7,5},{8,10},{9,11},{10,... | collective-permute-start | bytes 12582920 | tf_op jit(solution)/shard_map/ppermute | solution.py:175
  40.2 47.8 %collective-permute-start.10 = (bf16[4096,256]{1,0:T(8,128)(2,1)S(1)}, bf16[4096,256]{1,0:T(8,128)(2,1)S(1)}, u32[]{:S(2)}, u32[]{:S(2)}) collective-permute-start(bf16[4096,256]{1,0:T(8,128)(2,1)S(1)} %bitcast.142), channel_id=1, source_target_pairs={{0,4},{8,0},{16,8},{24,16},{28,24},{20,28},{12,20},{4,12},{1,5},{9... | collective-permute-start | bytes 6291464 | tf_op jit(solution)/shard_map/ppermute | solution.py:154
  42.5 47.2 %collective-permute-start.3 = (bf16[4096,256]{1,0:T(8,128)(2,1)S(1)}, bf16[4096,256]{1,0:T(8,128)(2,1)S(1)}, u32[]{:S(2)}, u32[]{:S(2)}) collective-permute-start(bf16[4096,256]{1,0:T(8,128)(2,1)S(1)} %bitcast.143), channel_id=1, source_target_pairs={{0,8},{8,16},{16,24},{24,28},{28,20},{20,12},{12,4},{4,0},{1,9},{9... | collective-permute-start | bytes 6291464 | tf_op jit(solution)/shard_map/ppermute | solution.py:154
  88.0 1.7 copy-start.11
  88.0 46.8 %collective-permute-start.11 = (bf16[4096,256]{1,0:T(8,128)(2,1)S(1)}, bf16[4096,256]{1,0:T(8,128)(2,1)}, u32[]{:S(2)}, u32[]{:S(2)}) collective-permute-start(bf16[4096,256]{1,0:T(8,128)(2,1)S(1)} %collective-permute-done.10.refs_4_), channel_id=1, source_target_pairs={{0,4},{8,0},{16,8},{24,16},{28,24},{20,28},{12,20},{4,12},{1,5},{9... | collective-permute-start | bytes 6291464 | tf_op jit(solution)/shard_map/ppermute | solution.py:154
  89.7 45.1 %copy-start.12 = (bf16[4096,256]{1,0:T(8,128)(2,1)}, bf16[4096,256]{1,0:T(8,128)(2,1)S(1)}, u32[]{:S(2)}) copy-start(bf16[4096,256]{1,0:T(8,128)(2,1)S(1)} %collective-permute-done.3.refs_4_) | copy-start | bytes 6291460
  89.7 46.5 %collective-permute-start.5 = (bf16[4096,256]{1,0:T(8,128)(2,1)S(1)}, bf16[4096,256]{1,0:T(8,128)(2,1)}, u32[]{:S(2)}, u32[]{:S(2)}) collective-permute-start(bf16[4096,256]{1,0:T(8,128)(2,1)S(1)} %collective-permute-done.3.refs_4_), channel_id=1, source_target_pairs={{0,8},{8,16},{16,24},{24,28},{28,20},{20,12},{12,4},{4,0},{1,9},{9... | collective-permute-start | bytes 6291464 | tf_op jit(solution)/shard_map/ppermute | solution.py:154
  91.1 119.8 %collective-permute-start.1 = (bf16[256,8192]{1,0:T(8,128)(2,1)}, bf16[256,8192]{1,0:T(8,128)(2,1)}, u32[]{:S(2)}, u32[]{:S(2)}) collective-permute-start(bf16[256,8192]{1,0:T(8,128)(2,1)} %bitcast.6.refs_0_), channel_id=1, source_target_pairs={{0,1},{1,0},{2,3},{3,2},{4,5},{5,4},{6,7},{7,6},{8,9},{9,8},{10,11... | collective-permute-start | bytes 12582920 | tf_op jit(solution)/shard_map/ppermute | solution.py:175
  132.1 78.8 %collective-permute-start.2 = (bf16[256,8192]{1,0:T(8,128)(2,1)}, bf16[256,8192]{1,0:T(8,128)(2,1)}, u32[]{:S(2)}, u32[]{:S(2)}) collective-permute-start(bf16[256,8192]{1,0:T(8,128)(2,1)} %collective-permute-done.refs_1_), channel_id=1, source_target_pairs={{0,1},{1,0},{2,3},{3,2},{4,5},{5,4},{6,7},{7,6},{8,9},{9,8},{10,11... | collective-permute-start | bytes 12582920 | tf_op jit(solution)/shard_map/ppermute | solution.py:175
  134.8 46.3 %collective-permute-start.12 = (bf16[4096,256]{1,0:T(8,128)(2,1)}, bf16[4096,256]{1,0:T(8,128)(2,1)}, u32[]{:S(2)}, u32[]{:S(2)}) collective-permute-start(bf16[4096,256]{1,0:T(8,128)(2,1)} %collective-permute-done.11.refs_4_), channel_id=1, source_target_pairs={{0,4},{8,0},{16,8},{24,16},{28,24},{20,28},{12,20},{4,12},{1,5},{9... | collective-permute-start | bytes 6291464 | tf_op jit(solution)/shard_map/ppermute | solution.py:154
  136.2 47.9 %collective-permute-start.7 = (bf16[4096,256]{1,0:T(8,128)(2,1)}, bf16[4096,256]{1,0:T(8,128)(2,1)}, u32[]{:S(2)}, u32[]{:S(2)}) collective-permute-start(bf16[4096,256]{1,0:T(8,128)(2,1)} %collective-permute-done.5.refs_4_), channel_id=1, source_target_pairs={{0,8},{8,16},{16,24},{24,28},{28,20},{20,12},{12,4},{4,0},{1,9},{9... | collective-permute-start | bytes 6291464 | tf_op jit(solution)/shard_map/ppermute | solution.py:154
  138.3 3.7 copy-start.3
  139.8 50.8 %copy-start.19 = (s32[8]{0:T(128)S(1)}, s32[8]{0:T(128)}, u32[]{:S(2)}) copy-start(s32[8]{0:T(128)} %constant.124.clone) | copy-start | bytes 100
  139.8 60.7 %copy-start.17 = (bf16[1,2,64,512]{3,2,1,0:T(8,128)(2,1)S(1)}, bf16[1,2,64,512]{3,2,1,0:T(8,128)(2,1)}, u32[]{:S(2)}) copy-start(bf16[1,2,64,512]{3,2,1,0:T(8,128)(2,1)} %param.17) | copy-start | bytes 393220
  182.4 24.2 %collective-permute-start.13 = (bf16[2048,256]{1,0:T(8,128)(2,1)S(1)}, bf16[2048,256]{1,0:T(8,128)(2,1)S(1)}, u32[]{:S(2)}, u32[]{:S(2)}) collective-permute-start(bf16[2048,256]{1,0:T(8,128)(2,1)S(1)} %slice.56), channel_id=1, source_target_pairs={{0,4},{8,0},{16,8},{24,16},{28,24},{20,28},{12,20},{4,12},{1,5},{9... | collective-permute-start | bytes 3145736 | tf_op jit(solution)/shard_map/ppermute | solution.py:154
  185.4 22.8 %collective-permute-start.9 = (bf16[2048,256]{1,0:T(8,128)(2,1)S(1)}, bf16[2048,256]{1,0:T(8,128)(2,1)}, u32[]{:S(2)}, u32[]{:S(2)}) collective-permute-start(bf16[2048,256]{1,0:T(8,128)(2,1)S(1)} %slice.55), channel_id=1, source_target_pairs={{0,8},{8,16},{16,24},{24,28},{28,20},{20,12},{12,4},{4,0},{1,9},{9... | collective-permute-start | bytes 3145736 | tf_op jit(solution)/shard_map/ppermute | solution.py:154
  231.4 64.8 %collective-permute-start.4 = (bf16[4,256,256]{2,1,0:T(8,128)(2,1)}, bf16[4,256,256]{2,1,0:T(8,128)(2,1)}, u32[]{:S(2)}, u32[]{:S(2)}) collective-permute-start(bf16[4,256,256]{2,1,0:T(8,128)(2,1)} %shard_map.140), channel_id=1, source_target_pairs={{0,4},{8,0},{16,8},{24,16},{28,24},{20,28},{12,20},{4,12},{1,5},{9... | collective-permute-start | bytes 1572872 | tf_op jit(solution)/shard_map/ppermute | solution.py:154
  242.3 56.0 %collective-permute-start.6 = (bf16[4,256,256]{2,1,0:T(8,128)(2,1)}, bf16[4,256,256]{2,1,0:T(8,128)(2,1)}, u32[]{:S(2)}, u32[]{:S(2)}) collective-permute-start(bf16[4,256,256]{2,1,0:T(8,128)(2,1)} %shard_map.141), channel_id=1, source_target_pairs={{0,12},{8,4},{16,0},{24,8},{28,16},{20,24},{12,28},{4,20},{1,13},{... | collective-permute-start | bytes 1572872 | tf_op jit(solution)/shard_map/ppermute | solution.py:154
  254.2 47.2 %collective-permute-start.8 = (bf16[4,256,256]{2,1,0:T(8,128)(2,1)}, bf16[4,256,256]{2,1,0:T(8,128)(2,1)S(1)}, u32[]{:S(2)}, u32[]{:S(2)}) collective-permute-start(bf16[4,256,256]{2,1,0:T(8,128)(2,1)} %shard_map.142), channel_id=1, source_target_pairs={{0,20},{8,12},{16,4},{24,0},{28,8},{20,16},{12,24},{4,28},{1,21},{... | collective-permute-start | bytes 1572872 | tf_op jit(solution)/shard_map/ppermute | solution.py:154
  263.8 47.5 %collective-permute-start.14 = (bf16[4,256,256]{2,1,0:T(8,128)(2,1)}, bf16[4,256,256]{2,1,0:T(8,128)(2,1)S(1)}, u32[]{:S(2)}, u32[]{:S(2)}) collective-permute-start(bf16[4,256,256]{2,1,0:T(8,128)(2,1)} %shard_map.143), channel_id=1, source_target_pairs={{0,28},{8,20},{16,12},{24,4},{28,0},{20,8},{12,16},{4,24},{1,29},{... | collective-permute-start | bytes 1572872 | tf_op jit(solution)/shard_map/ppermute | solution.py:154
  267.3 63.7 %collective-permute-start.21 = (bf16[8,2,64,512]{3,2,1,0:T(8,128)(2,1)}, bf16[8,2,64,512]{3,2,1,0:T(8,128)(2,1)}, u32[]{:S(2)}, u32[]{:S(2)}) collective-permute-start(bf16[8,2,64,512]{3,2,1,0:T(8,128)(2,1)} %bitcast.3.child_ref), channel_id=1, source_target_pairs={{0,2},{1,3},{2,0},{3,1},{4,6},{5,7},{6,4},{7,5},{8,10},{9,11},{10,... | collective-permute-start | bytes 3145736 | tf_op jit(solution)/shard_map/ppermute | solution.py:188
  286.7 9.5 %copy-start.15 = (bf16[4,256,256]{2,1,0:T(8,128)(2,1)S(1)}, bf16[4,256,256]{2,1,0:T(8,128)(2,1)}, u32[]{:S(2)}) copy-start(bf16[4,256,256]{2,1,0:T(8,128)(2,1)} %shard_map.144) | copy-start | bytes 1572868
  286.8 11.6 %copy-start.6 = (bf16[1,8,2,64,512]{4,3,2,1,0:T(8,128)(2,1)S(1)}, bf16[1,8,2,64,512]{4,3,2,1,0:T(8,128)(2,1)}, u32[]{:S(2)}) copy-start(bf16[1,8,2,64,512]{4,3,2,1,0:T(8,128)(2,1)} %param.15) | copy-start | bytes 3145732
  286.8 14.6 %copy-start.14 = (bf16[4,256,256]{2,1,0:T(8,128)(2,1)S(1)}, bf16[4,256,256]{2,1,0:T(8,128)(2,1)}, u32[]{:S(2)}) copy-start(bf16[4,256,256]{2,1,0:T(8,128)(2,1)} %shard_map.145) | copy-start | bytes 1572868
  296.2 34.8 %collective-permute-start.15 = (bf16[4,256,256]{2,1,0:T(8,128)(2,1)S(1)}, bf16[4,256,256]{2,1,0:T(8,128)(2,1)S(1)}, u32[]{:S(2)}, u32[]{:S(2)}) collective-permute-start(bf16[4,256,256]{2,1,0:T(8,128)(2,1)S(1)} %copy-done.15), channel_id=1, source_target_pairs={{0,24},{8,28},{16,20},{24,12},{28,4},{20,0},{12,8},{4,16},{1,25},{... | collective-permute-start | bytes 1572872 | tf_op jit(solution)/shard_map/ppermute | solution.py:154
  298.3 45.3 %collective-permute-start.18 = (bf16[8,2,64,512]{3,2,1,0:T(8,128)(2,1)S(1)}, bf16[8,2,64,512]{3,2,1,0:T(8,128)(2,1)}, u32[]{:S(2)}, u32[]{:S(2)}) collective-permute-start(bf16[8,2,64,512]{3,2,1,0:T(8,128)(2,1)S(1)} %bitcast.149), channel_id=1, source_target_pairs={{0,2},{1,3},{2,0},{3,1},{4,6},{5,7},{6,4},{7,5},{8,10},{9,11},{10,... | collective-permute-start | bytes 3145736 | tf_op jit(solution)/shard_map/ppermute | solution.py:188
  301.4 41.4 %collective-permute-start.16 = (bf16[4,256,256]{2,1,0:T(8,128)(2,1)S(1)}, bf16[4,256,256]{2,1,0:T(8,128)(2,1)S(1)}, u32[]{:S(2)}, u32[]{:S(2)}) collective-permute-start(bf16[4,256,256]{2,1,0:T(8,128)(2,1)S(1)} %copy-done.14), channel_id=1, source_target_pairs={{0,16},{8,24},{16,28},{24,20},{28,12},{20,4},{12,0},{4,8},{1,17},{... | collective-permute-start | bytes 1572872 | tf_op jit(solution)/shard_map/ppermute | solution.py:154
  311.3 32.8 %collective-permute-start.17 = (bf16[4,256,256]{2,1,0:T(8,128)(2,1)}, bf16[4,256,256]{2,1,0:T(8,128)(2,1)S(1)}, u32[]{:S(2)}, u32[]{:S(2)}) collective-permute-start(bf16[4,256,256]{2,1,0:T(8,128)(2,1)} %shard_map.146), channel_id=1, source_target_pairs={{0,8},{8,16},{16,24},{24,28},{28,20},{20,12},{12,4},{4,0},{1,9},{9... | collective-permute-start | bytes 1572872 | tf_op jit(solution)/shard_map/ppermute | solution.py:154
  331.0 26.7 %collective-permute-start.22 = (bf16[8,2,64,512]{3,2,1,0:T(8,128)(2,1)}, bf16[8,2,64,512]{3,2,1,0:T(8,128)(2,1)}, u32[]{:S(2)}, u32[]{:S(2)}) collective-permute-start(bf16[8,2,64,512]{3,2,1,0:T(8,128)(2,1)} %bitcast.3.child_ref), channel_id=1, source_target_pairs={{0,1},{1,0},{2,3},{3,2},{4,5},{5,4},{6,7},{7,6},{8,9},{9,8},{10,11... | collective-permute-start | bytes 3145736 | tf_op jit(solution)/shard_map/ppermute | solution.py:188
  331.0 26.7 %collective-permute-start.23 = (bf16[8,2,64,512]{3,2,1,0:T(8,128)(2,1)}, bf16[8,2,64,512]{3,2,1,0:T(8,128)(2,1)}, u32[]{:S(2)}, u32[]{:S(2)}) collective-permute-start(bf16[8,2,64,512]{3,2,1,0:T(8,128)(2,1)} %collective-permute-done.21), channel_id=1, source_target_pairs={{0,1},{1,0},{2,3},{3,2},{4,5},{5,4},{6,7},{7,6},{8,9},{9,8},{10,11... | collective-permute-start | bytes 3145736 | tf_op jit(solution)/shard_map/ppermute | solution.py:188
  342.7 30.3 %collective-permute-start.19 = (bf16[8,2,64,512]{3,2,1,0:T(8,128)(2,1)S(1)}, bf16[8,2,64,512]{3,2,1,0:T(8,128)(2,1)}, u32[]{:S(2)}, u32[]{:S(2)}) collective-permute-start(bf16[8,2,64,512]{3,2,1,0:T(8,128)(2,1)S(1)} %bitcast.150), channel_id=1, source_target_pairs={{0,1},{1,0},{2,3},{3,2},{4,5},{5,4},{6,7},{7,6},{8,9},{9,8},{10,11... | collective-permute-start | bytes 3145736 | tf_op jit(solution)/shard_map/ppermute | solution.py:188
  343.6 29.5 %collective-permute-start.20 = (bf16[8,2,64,512]{3,2,1,0:T(8,128)(2,1)}, bf16[8,2,64,512]{3,2,1,0:T(8,128)(2,1)}, u32[]{:S(2)}, u32[]{:S(2)}) collective-permute-start(bf16[8,2,64,512]{3,2,1,0:T(8,128)(2,1)} %collective-permute-done.18), channel_id=1, source_target_pairs={{0,1},{1,0},{2,3},{3,2},{4,5},{5,4},{6,7},{7,6},{8,9},{9,8},{10,11... | collective-permute-start | bytes 3145736 | tf_op jit(solution)/shard_map/ppermute | solution.py:188
  347.8 1.8 copy-start.4
  351.1 42.4 %all-to-all-start.1 = ((bf16[2,8,2,4,64,128]{5,4,2,1,0,3:T(8,128)(2,1)}), bf16[2,8,2,4,64,128]{5,4,2,1,0,3:T(8,128)(2,1)S(1)}, u32[]{:S(2)}, u32[]{:S(2)}) async-start(bf16[2,8,2,4,64,128]{5,4,2,1,0,3:T(8,128)(2,1)} %copy.37), calls=%async_computation.1 | async-start | bytes 4194304 | tf_op jit(solution)/shard_map/all_to_all | solution.py:233
  376.7 5.1 %copy-start.16 = (f32[128,512]{0,1:T(8,128)S(1)}, f32[128,512]{0,1:T(8,128)}, u32[]{:S(2)}) copy-start(f32[128,512]{0,1:T(8,128)} %copy.39) | copy-start | bytes 786436
  381.8 4.6 %copy-start.9 = (bf16[1,2,4,64,512]{4,3,1,0,2:T(8,128)(2,1)S(1)}, bf16[1,2,4,64,512]{4,3,1,0,2:T(8,128)(2,1)}, u32[]{:S(2)}) copy-start(bf16[1,2,4,64,512]{4,3,1,0,2:T(8,128)(2,1)} %slice.60) | copy-start | bytes 1572868
  381.8 5.4 %copy-start.8 = (bf16[7,512,128]{2,1,0:T(8,128)(2,1)S(1)}, bf16[7,512,128]{2,1,0:T(8,128)(2,1)}, u32[]{:S(2)}) copy-start(bf16[7,512,128]{2,1,0:T(8,128)(2,1)} %gather_fusion.5) | copy-start | bytes 2752516
  393.5 19.0 %all-to-all-start.2 = ((bf16[2,4,64,128]{3,2,0,1:T(8,128)(2,1)}), bf16[2,4,64,128]{3,2,0,1:T(8,128)(2,1)S(1)}, u32[]{:S(2)}, u32[]{:S(2)}) async-start(bf16[2,4,64,128]{3,2,0,1:T(8,128)(2,1)} %copy.41), calls=%async_computation.2 | async-start | bytes 262144 | tf_op jit(solution)/shard_map/all_to_all | solution.py:233
  402.5 4.9 %copy-start.10 = (bf16[1,2,4,64,512]{4,3,2,1,0:T(8,128)(2,1)S(1)}, bf16[1,2,4,64,512]{4,3,2,1,0:T(8,128)(2,1)}, u32[]{:S(2)}) copy-start(bf16[1,2,4,64,512]{4,3,2,1,0:T(8,128)(2,1)} %copy.45) | copy-start | bytes 1572868
  404.3 7.3 %copy-start.7 = (bf16[16,64,512]{2,1,0:T(8,128)(2,1)}, bf16[16,64,512]{2,1,0:T(8,128)(2,1)S(1)}, u32[]{:S(2)}) copy-start(bf16[16,64,512]{2,1,0:T(8,128)(2,1)S(1)} %get-tuple-element.20) | copy-start | bytes 3145732
  409.5 6.5 %copy-start.13 = (f32[2,64,512]{2,1,0:T(8,128)S(1)}, f32[2,64,512]{2,1,0:T(8,128)}, u32[]{:S(2)}) copy-start(f32[2,64,512]{2,1,0:T(8,128)} %fusion.40) | copy-start | bytes 786436
  409.5 16.0 %copy-start.1 = (s32[32]{0:T(128)S(1)}, s32[32]{0:T(128)}, u32[]{:S(2)}) copy-start(s32[32]{0:T(128)} %param.12) | copy-start | bytes 388
  411.6 13.2 %copy-start.18 = (bf16[1,2,64,512]{3,2,1,0:T(8,128)(2,1)S(1)}, bf16[1,2,64,512]{3,2,1,0:T(8,128)(2,1)}, u32[]{:S(2)}) copy-start(bf16[1,2,64,512]{3,2,1,0:T(8,128)(2,1)} %param.18) | copy-start | bytes 393220
  412.5 12.3 %all-to-all-start.3 = ((bf16[2,4,64,512]{3,2,0,1:T(8,128)(2,1)}), bf16[2,4,64,512]{3,2,0,1:T(8,128)(2,1)S(1)}, u32[]{:S(2)}, u32[]{:S(2)}) async-start(bf16[2,4,64,512]{3,2,0,1:T(8,128)(2,1)} %copy.46), calls=%async_computation.3 | async-start | bytes 1048576 | tf_op jit(solution)/shard_map/all_to_all | solution.py:272
